TPU v7x, 32 devices: a whole 2x2x4 slice. The times are simulated.
32 devices in a mesh: gx: 8 (over z, y), gy: 4 (over x, core).
Axes of the slice: x: 2, y: 2, z: 4, core: 2. Of those that a mesh axis runs over, the one named last changes fastest.
Arguments:
- coarse_send: bfloat16 [8, 35, 4096], P('gx', None, 'gy'), may hold values from -6 to 6
- coarse_flux: float32 [8, 35, 1024], P('gx', None, 'gy'), may hold values from -6 to 6
- patch_owner: int32 [8], replicated, may hold values from 0 to 15, as said below
- velocity: float32 [3], replicated, may hold values from -0.6 to 0.6
- diffusivity: float32 [35], replicated, may hold values from 0.03 to 0.15
- stoich: float32 [35, 35], replicated, may hold values from -1 to 1
Outputs:
- fine_state: float32 [16, 35, 32768], P('gx', None, 'gy')
- reflux: float32 [8, 35, 1024], P('gx', None, 'gy')
Inputs may be any that keep to these rules, and one draw needn't show every extreme that they name: `patch_owner`: the 8 entries are distinct; slot s belongs to owner group s // 2, the group of index s // 2 along gx; a group owns 0, 1 or 2 patches, and at least one group owns exactly 2.
All inputs are finite; a program needn't handle non-finite values.
Results may differ from a plain program's by a relative error of at most 0.0003.
Values may be sent and summed in bfloat16 or wider, within the bound.
No kernel may reach another device: no remote copies, remote signals or barrier semaphores. Data moves between devices by JAX's collectives and lax.ppermute only.
A program may use at most 128 MiB of HBM per device.

v0:
```python
import jax
import jax.numpy as jnp
from jax import lax
from jax.sharding import PartitionSpec as P

CB = 16


time_step = 0.25
heat_gain = 2.0
highest = lax.Precision.HIGHEST


def padded(block, sides, width):
    for axis, dim in sides:
        count = lax.axis_size(axis)
        forward = [(i, i + 1) for i in range(count - 1)]
        backward = [(target, source) for source, target in forward]
        low = lax.ppermute(
            lax.slice_in_dim(block, block.shape[dim] - width, None, axis=dim), axis, forward
        )
        high = lax.ppermute(lax.slice_in_dim(block, 0, width, axis=dim), axis, backward)
        block = jnp.concatenate([low, block, high], axis=dim)
    return block


def axis_slope(values, axis):
    moved = jnp.moveaxis(values, axis, 0)
    middle = (moved[2:] - moved[:-2]) * 0.5
    joined = jnp.concatenate([moved[1:2] - moved[0:1], middle, moved[-1:] - moved[-2:-1]], 0)
    return jnp.moveaxis(joined, 0, axis)


def spread(values):
    return values[..., :, None, :, None, :, None]


def refine(coarse, slope_z, slope_y, slope_x):
    offsets = jnp.array([-0.5, 0.5], jnp.float32)
    leading = coarse.shape[:-3]
    depth, height, breadth = coarse.shape[-3:]
    shift_y = offsets[:, None, None]
    shift_z = offsets[:, None, None, None, None]
    terms = spread(slope_x) * offsets + spread(slope_y) * shift_y + spread(slope_z) * shift_z
    fine_cells = spread(coarse) + terms * 0.5
    return fine_cells.reshape(leading + (2 * depth, 2 * height, 2 * breadth))


def face_flux(left_side, right_side, speed, diffuse):
    return speed * (left_side + right_side) * 0.5 - diffuse * (right_side - left_side)


def tendency(padded_layers, cells, velocity, diffusivity, stoich):
    diffuse = diffusivity[:, None, None, None]
    padded_cols = jnp.concatenate([cells[..., :1], cells, cells[..., -1:]], -1)
    padded_rows = jnp.concatenate([cells[..., :1, :], cells, cells[..., -1:, :]], -2)
    flux_cols = face_flux(padded_cols[..., :-1], padded_cols[..., 1:], velocity[0], diffuse)
    flux_rows = face_flux(padded_rows[..., :-1, :], padded_rows[..., 1:, :], velocity[1], diffuse)
    flux_layers = face_flux(
        padded_layers[..., :-1, :, :], padded_layers[..., 1:, :, :], velocity[2], diffuse
    )
    outflow = (
        flux_cols[..., 1:]
        - flux_cols[..., :-1]
        + (flux_rows[..., 1:, :] - flux_rows[..., :-1, :])
        + (flux_layers[..., 1:, :, :] - flux_layers[..., :-1, :, :])
    )
    reaction_rate = cells * jax.nn.sigmoid(heat_gain * cells[..., 0:1, :, :, :])
    source = jnp.einsum("fg,...gzyx->...fzyx", stoich, reaction_rate, precision=highest)
    side_fluxes = (
        flux_cols[..., 0],
        flux_cols[..., -1],
        flux_rows[..., 0, :],
        flux_rows[..., -1, :],
    )
    return (source - outflow, side_fluxes)


def tendency_slots(padded_layers, cells, velocity, diffusivity, stoich):

    def tendency_one_slot(pair):
        return tendency(pair[0], pair[1], velocity, diffusivity, stoich)

    return lax.map(tendency_one_slot, (padded_layers, cells))


def refine_slots(coarse, slope_z):

    def refine_one_slot(pair):
        block, slope_layers = pair
        return refine(block, slope_layers, axis_slope(block, 2), axis_slope(block, 3))

    return lax.map(refine_one_slot, (coarse, slope_z))


def average_sides(earlier, later_sides):
    return jnp.stack(
        [
            (earlier[0] + later_sides[0]) * 0.5,
            (earlier[1] + later_sides[1]) * 0.5,
            (earlier[2] + later_sides[2]) * 0.5,
            (earlier[3] + later_sides[3]) * 0.5,
        ],
        -2,
    )


def coarsen_faces(register):
    leading = register.shape[:-3]
    depth = register.shape[-3] // 2
    along = register.shape[-1] // 2
    split_faces = register.reshape(leading + (depth, 2, 4, along, 2))
    return (
        split_faces[..., 0, :, :, 0]
        + split_faces[..., 0, :, :, 1]
        + split_faces[..., 1, :, :, 0]
        + split_faces[..., 1, :, :, 1]
    ) * 0.25


def route_home(values, patch_owner, my_slots):
    chooser = (patch_owner[:, None] == my_slots[None, :]).astype(jnp.float32)
    return jnp.einsum("qo,ofc->qfc", chooser, values, precision=highest)


def shards(coarse_send, coarse_flux, patch_owner, velocity, diffusivity, stoich):
    send_slots, fields, layer_cells = coarse_send.shape
    own_slots = 2 * send_slots
    owner_group = lax.axis_index("gx")
    pencil = lax.axis_index("gy")
    pencils = lax.axis_size("gy")
    block_edge = CB
    layers = layer_cells // (block_edge * block_edge)
    my_slots = owner_group * own_slots + jnp.arange(own_slots, dtype=jnp.int32)
    chooser = (my_slots[:, None] == patch_owner[None, :]).astype(jnp.bfloat16)
    gathered = jnp.einsum(
        "oq,qfc->ofc",
        chooser,
        lax.all_gather(coarse_send, "gx", axis=0, tiled=True),
        preferred_element_type=jnp.float32,
    )
    coarse = gathered.reshape(own_slots, fields, layers, block_edge, block_edge)
    rimmed = padded(coarse.astype(jnp.bfloat16), (("gy", 2),), 1).astype(coarse.dtype)
    below = rimmed[:, :, :-2]
    above = rimmed[:, :, 2:]
    depth_index = pencil * layers + jnp.arange(layers, dtype=jnp.int32)
    is_first = (depth_index == 0)[:, None, None]
    is_last = (depth_index == block_edge - 1)[:, None, None]
    slope_z = jnp.where(
        is_first, above - coarse, jnp.where(is_last, coarse - below, (above - below) * 0.5)
    )
    fine_cells = refine_slots(coarse, slope_z)
    at_bottom = pencil == 0
    at_top = pencil == pencils - 1

    def extend_layers(cells):
        ghosts = padded(cells.astype(jnp.bfloat16), (("gy", 2),), 1).astype(cells.dtype)
        lower_ghost = jnp.where(at_bottom, cells[:, :, :1], ghosts[:, :, :1])
        upper_ghost = jnp.where(at_top, cells[:, :, -1:], ghosts[:, :, -1:])
        return jnp.concatenate([lower_ghost, cells, upper_ghost], 2)

    change, first_sides = tendency_slots(
        extend_layers(fine_cells), fine_cells, velocity, diffusivity, stoich
    )
    section_state = fine_cells + time_step * change
    second, second_sides = tendency_slots(
        extend_layers(section_state), section_state, velocity, diffusivity, stoich
    )
    final_state = fine_cells + time_step * 0.5 * (change + second)
    register = average_sides(first_sides, second_sides)
    flat_faces = coarsen_faces(register).reshape(own_slots, fields, -1)
    summed = lax.psum_scatter(
        route_home(flat_faces, patch_owner, my_slots), "gx", scatter_dimension=0, tiled=True
    )
    averaged = summed.reshape(send_slots, fields, layers, 4, block_edge)
    corrected = averaged - coarse_flux.reshape(send_slots, fields, layers, 4, block_edge)
    return (final_state.reshape(own_slots, fields, -1), corrected.reshape(send_slots, fields, -1))


def solution(mesh):
    placed = (P("gx", None, "gy"), P("gx", None, "gy"), P(), P(), P(), P())
    return jax.shard_map(
        shards,
        mesh=mesh,
        in_specs=placed,
        out_specs=(P("gx", None, "gy"), P("gx", None, "gy")),
        check_vma=False,
    )
```

profile of v0, /device:TPU:1, one launch (start us, length us, event | category | flops | bytes accessed | tf_op | source)
XLA Modules:
  0.0 390.0 jit_solution(8805554592416697023)
XLA Ops:
  7.2 27.5 %all_gather.3 = bf16[8,35,1024]{2,1,0:T(8,128)(2,1)S(1)} all-gather(bf16[1,35,1024]{2,1,0:T(8,128)(2,1)} %param.13), channel_id=1, replica_groups=mesh['gx'=8,'gy'=4] {'gx'}, dimensions={0}, use_global_device_ids=true | all-gather | bytes 645120 | tf_op jit(solution)/shard_map/all_gather | solution.py:139
  36.3 9.2 %collective-permute-start = (bf16[2,35,1,16,16]{1,4,3,2,0:T(8,128)(2,1)S(1)}, bf16[2,35,1,16,16]{1,4,3,2,0:T(8,128)(2,1)S(1)}, u32[]{:S(2)}, u32[]{:S(2)}) collective-permute-start(bf16[2,35,1,16,16]{1,4,3,2,0:T(8,128)(2,1)S(1)} %get-tuple-element.340), channel_id=1, source_target_pairs={{0,1},{1,2},{2,3},{4,5},{5,6},{6,7},{8,9},{9,10},{10,11},{12,13},{... | collective-permute-start | bytes 107528 | tf_op jit(solution)/shard_map/ppermute | solution.py:19
  47.5 4.3 %collective-permute-done.1 = bf16[2,35,1,16,16]{1,4,3,2,0:T(8,128)(2,1)S(1)} collective-permute-done((bf16[2,35,1,16,16]{1,4,3,2,0:T(8,128)(2,1)S(1)}, bf16[2,35,1,16,16]{1,4,3,2,0:T(8,128)(2,1)S(1)}, u32[]{:S(2)}, u32[]{:S(2)}) %collective-permute-start.1) | collective-permute-done | bytes 35872 | tf_op jit(solution)/shard_map/ppermute | solution.py:22
  52.3 4.5 %broadcast.182.clone = f32[2,35,8,32,32]{1,4,3,2,0:T(8,128)} broadcast(f32[]{:T(128)} %constant.54.clone.1), dimensions={} | broadcast | bytes 2293764 | tf_op jit(solution)/shard_map/broadcast.31
  56.8 17.1 %while.49 = (s32[]{:T(128)}, f32[2,35,8,32,32]{1,4,3,2,0:T(8,128)}, f32[2,35,4,16,16]{1,4,3,2,0:T(8,128)S(1)}, f32[2,35,4,16,16]{1,4,3,2,0:T(8,128)S(1)}, s32[]{:T(128)}, /*index=5*/f32[2]{0:T(128)S(1)}) while((s32[]{:T(128)}, f32[2,35,8,32,32]{1,4,3,2,0:T(8,128)}, f32[2,35,4,16,16]{1,4,3,2,0:T(8,128)S(1)}, ...), condition=%wide.region_1.2_spmd.clone, body=%wide.region_0.1_spmd.sunk.clone.sunk | while | flops 1496322 | bytes 12653153 | solution.py:93
  62.6 2.8 constant_dynamic-update-slice_fusion.10
  71.1 2.8 constant_dynamic-update-slice_fusion.10
  73.9 4.5 %convert_element_type.22 = bf16[2,35,8,32,32]{1,4,3,2,0:T(8,128)(2,1)S(1)} convert(f32[2,35,8,32,32]{1,4,3,2,0:T(8,128)} %get-tuple-element.589) | non-fusion elementwise | flops 573440 | bytes 3440640 | tf_op jit(solution)/shard_map/convert_element_type | solution.py:157
  84.9 3.7 collective-permute-done.2
  88.6 4.4 %collective-permute-done.3 = bf16[2,35,1,32,32]{1,4,3,2,0:T(8,128)(2,1)S(1)} collective-permute-done((bf16[2,35,1,32,32]{1,4,3,2,0:T(8,128)(2,1)S(1)}, bf16[2,35,1,32,32]{1,4,3,2,0:T(8,128)(2,1)S(1)}, u32[]{:S(2)}, u32[]{:S(2)}) %collective-permute-start.3) | collective-permute-done | bytes 143392 | tf_op jit(solution)/shard_map/ppermute | solution.py:22
  94.9 9.3 %pad_maximum_fusion.8 = f32[2,35,10,32,32]{1,4,3,2,0:T(8,128)} fusion(f32[2,35,1,32,32]{1,4,3,2,0:T(8,128)S(1)} %get-tuple-element.335, f32[2,35,8,32,32]{1,4,3,2,0:T(8,128)} %get-tuple-element.589, f32[2,35,1,32,32]{1,4,3,2,0:T(8,128)S(1)} %get-tuple-element.334), kind=kLoop, calls=%fused_computation.78 | loop fusion | flops 1433600 | bytes 5734400 | tf_op jit(solution)/shard_map/concatenate | solution.py:160
  104.1 4.4 %broadcast.182.clone.1 = f32[2,35,8,32,32]{1,4,3,2,0:T(8,128)} broadcast(f32[]{:T(128)} %constant.54.clone.1), dimensions={} | broadcast | bytes 2293764 | tf_op jit(solution)/shard_map/broadcast.31
  108.6 81.6 %while.47 = (s32[]{:T(128)}, f32[2,35,8,32,32]{1,4,3,2,0:T(8,128)}, f32[2,35,8,32]{1,3,2,0:T(8,128)S(1)}, f32[2,35,8,32]{1,3,2,0:T(8,128)S(1)}, f32[2,35,8,32]{1...) while((s32[]{:T(128)}, f32[2,35,8,32,32]{1,4,3,2,0:T(8,128)}, ...), condition=%wide.region_3.4_spmd, body=%wide.region_2.3_spmd.sunk | while | flops 129128448 | bytes 80370104 | solution.py:84
  108.8 2.9 dynamic-slice_bitcast_fusion.15
  112.7 4.4 %multiply_subtract_fusion.14 = f32[35,8,32,33]{0,3,2,1:T(8,128)} fusion(f32[35,8,32,1]{0,3,2,1:T(1,128)S(1)} %get-tuple-element.523, f32[35,8,32,32]{0,3,2,1:T(8,128)S(1)} %dynamic-slice_bitcast_fusion.15, f32[35,8,32,1]{0,3,2,1:T(1,128)S(1)} %get-tuple-element.524, f32[35]{0:T(128)S(1)} %get-tuple-element.616, f32[]{:T(128)} %bitcast.137), kind=kLoop, calls=%fused_computation.3.clone.1 | loop fusion | flops 2365440 | bytes 2401424 | tf_op jit(solution)/shard_map/while/body/eval_jaxpr/sub | solution.py:50
  117.1 3.4 multiply_subtract_fusion.13
  121.2 3.7 multiply_subtract_fusion.12
  124.8 4.6 %constant_dynamic-slice_fusion.4 = f32[1,1,8,32,32]{1,4,3,2,0:T(8,128)} fusion(f32[2,35,8,32,32]{1,4,3,2,0:T(8,128)} %get-tuple-element.613, s32[]{:T(128)} %get-tuple-element.595), kind=kLoop, calls=%fused_computation.26.clone.1 | loop fusion | bytes 65540 | tf_op jit(solution)/shard_map/while/body/eval_jaxpr/slice | solution.py:68
  129.4 3.2 copy.80
  132.7 14.0 %fusion.78 = f32[2,35,8,32,32]{1,4,3,2,0:T(8,128)} fusion(f32[2,35,8,32,32]{1,4,3,2,0:T(8,128)} %get-tuple-element.596, s32[]{:T(128)} %get-tuple-element.595, f32[35,9,32,32]{0,3,2,1:T(8,128)} %multiply_subtract_fusion.12, f32[35,8,33,32]{0,3,2,1:T(8,128)} %multiply_subtract_fusion.13, f32[35,8,32,33]{0,3,2,1:T(8,128)} %multiply_subtract_fusion.14, ...), kind=kOutput, calls=%fused_computation.12.clone.1 | convolution fusion | flops 122429440 | bytes 33593124 | tf_op jit(solution)/shard_map/while/body/eval_jaxpr/fg,...gzyx->...fzyx/dot_general | solution.py:69
  149.5 2.9 dynamic-slice_bitcast_fusion.15
  153.4 4.4 %multiply_subtract_fusion.14 = f32[35,8,32,33]{0,3,2,1:T(8,128)} fusion(f32[35,8,32,1]{0,3,2,1:T(1,128)S(1)} %get-tuple-element.523, f32[35,8,32,32]{0,3,2,1:T(8,128)S(1)} %dynamic-slice_bitcast_fusion.15, f32[35,8,32,1]{0,3,2,1:T(1,128)S(1)} %get-tuple-element.524, f32[35]{0:T(128)S(1)} %get-tuple-element.616, f32[]{:T(128)} %bitcast.137), kind=kLoop, calls=%fused_computation.3.clone.1 | loop fusion | flops 2365440 | bytes 2401424 | tf_op jit(solution)/shard_map/while/body/eval_jaxpr/sub | solution.py:50
  157.8 3.4 multiply_subtract_fusion.13
  161.8 3.7 multiply_subtract_fusion.12
  165.5 4.6 %constant_dynamic-slice_fusion.4 = f32[1,1,8,32,32]{1,4,3,2,0:T(8,128)} fusion(f32[2,35,8,32,32]{1,4,3,2,0:T(8,128)} %get-tuple-element.613, s32[]{:T(128)} %get-tuple-element.595), kind=kLoop, calls=%fused_computation.26.clone.1 | loop fusion | bytes 65540 | tf_op jit(solution)/shard_map/while/body/eval_jaxpr/slice | solution.py:68
  170.1 3.2 copy.80
  173.4 14.1 %fusion.78 = f32[2,35,8,32,32]{1,4,3,2,0:T(8,128)} fusion(f32[2,35,8,32,32]{1,4,3,2,0:T(8,128)} %get-tuple-element.596, s32[]{:T(128)} %get-tuple-element.595, f32[35,9,32,32]{0,3,2,1:T(8,128)} %multiply_subtract_fusion.12, f32[35,8,33,32]{0,3,2,1:T(8,128)} %multiply_subtract_fusion.13, f32[35,8,32,33]{0,3,2,1:T(8,128)} %multiply_subtract_fusion.14, ...), kind=kOutput, calls=%fused_computation.12.clone.1 | convolution fusion | flops 122429440 | bytes 33593124 | tf_op jit(solution)/shard_map/while/body/eval_jaxpr/fg,...gzyx->...fzyx/dot_general | solution.py:69
  190.2 12.9 %fusion.42 = (bf16[2,35,8,32,32]{1,4,3,2,0:T(8,128)(2,1)}, f32[2,35,8,32,32]{1,4,3,2,0:T(8,128)}) fusion(f32[2,35,8,32,32]{1,4,3,2,0:T(8,128)} %get-tuple-element.589, f32[2,35,8,32,32]{1,4,3,2,0:T(8,128)} %get-tuple-element.152), kind=kLoop, calls=%fused_computation.120 | loop fusion | flops 1720320 | bytes 8028160 | tf_op jit(solution)/shard_map/convert_element_type | solution.py:157
  210.3 3.3 collective-permute-done.4
  213.6 4.1 %collective-permute-done.5 = bf16[2,35,1,32,32]{1,4,3,2,0:T(8,128)(2,1)S(1)} collective-permute-done((bf16[2,35,1,32,32]{1,4,3,2,0:T(8,128)(2,1)S(1)}, bf16[2,35,1,32,32]{1,4,3,2,0:T(8,128)(2,1)S(1)}, u32[]{:S(2)}, u32[]{:S(2)}) %collective-permute-start.5) | collective-permute-done | bytes 143392 | tf_op jit(solution)/shard_map/ppermute | solution.py:22
  221.7 5.8 %pad_maximum_fusion.9 = f32[2,35,10,32,32]{1,4,3,2,0:T(8,128)} fusion(f32[2,35,1,32,32]{1,4,3,2,0:T(8,128)S(1)} %get-tuple-element.333, f32[2,35,8,32,32]{1,4,3,2,0:T(8,128)S(1)} %copy-done, f32[2,35,1,32,32]{1,4,3,2,0:T(8,128)S(1)} %get-tuple-element.332), kind=kLoop, calls=%fused_computation.79 | loop fusion | flops 1433600 | bytes 5734400 | tf_op jit(solution)/shard_map/concatenate | solution.py:160
  227.5 4.4 %broadcast.182 = f32[2,35,8,32,32]{1,4,3,2,0:T(8,128)} broadcast(f32[]{:T(128)} %constant.54.clone.1), dimensions={} | broadcast | bytes 2293764 | tf_op jit(solution)/shard_map/broadcast.31
  232.0 78.0 %while.48 = (s32[]{:T(128)}, f32[2,35,8,32,32]{1,4,3,2,0:T(8,128)}, f32[2,35,8,32]{1,3,2,0:T(8,128)S(1)}, f32[2,35,8,32]{1,3,2,0:T(8,128)S(1)}, f32[2,35,8,32]{1...) while((s32[]{:T(128)}, f32[2,35,8,32,32]{1,4,3,2,0:T(8,128)}, ...), condition=%wide.region_5.6_spmd, body=%wide.region_4.5_spmd.sunk | while | flops 129128448 | bytes 105535960 | solution.py:84
  232.2 2.9 dynamic-slice_bitcast_fusion.17
  236.0 4.4 %multiply_subtract_fusion.17 = f32[35,8,32,33]{0,3,2,1:T(8,128)} fusion(f32[35,8,32,1]{0,3,2,1:T(1,128)S(1)} %get-tuple-element.546, f32[35,8,32,32]{0,3,2,1:T(8,128)S(1)} %dynamic-slice_bitcast_fusion.17, f32[35,8,32,1]{0,3,2,1:T(1,128)S(1)} %get-tuple-element.547, f32[35]{0:T(128)S(1)} %get-tuple-element.652, f32[]{:T(128)} %bitcast.150), kind=kLoop, calls=%fused_computation.32.clone.1 | loop fusion | flops 2365440 | bytes 2401424 | tf_op jit(solution)/shard_map/while/body/eval_jaxpr/sub | solution.py:50
  240.5 3.3 multiply_subtract_fusion.16
  244.4 4.1 %multiply_subtract_fusion.15 = f32[35,9,32,32]{0,3,2,1:T(8,128)} fusion(f32[35,10,32,32]{0,3,2,1:T(8,128)S(1)} %dynamic-slice_bitcast_fusion.16, f32[35]{0:T(128)S(1)} %get-tuple-element.652, f32[]{:T(128)} %bitcast.148), kind=kLoop, calls=%fused_computation.33.clone.1 | loop fusion | flops 1935360 | bytes 3870864 | tf_op jit(solution)/shard_map/while/body/eval_jaxpr/sub | solution.py:50
  251.0 3.2 copy.81
  254.3 14.1 %fusion.86 = f32[2,35,8,32,32]{1,4,3,2,0:T(8,128)} fusion(f32[2,35,8,32,32]{1,4,3,2,0:T(8,128)} %get-tuple-element.632, s32[]{:T(128)} %get-tuple-element.631, f32[35,9,32,32]{0,3,2,1:T(8,128)} %multiply_subtract_fusion.15, f32[35,8,33,32]{0,3,2,1:T(8,128)} %multiply_subtract_fusion.16, f32[35,8,32,33]{0,3,2,1:T(8,128)} %multiply_subtract_fusion.17, ...), kind=kOutput, calls=%fused_computation.41.clone.1 | convolution fusion | flops 122429440 | bytes 33593124 | tf_op jit(solution)/shard_map/while/body/eval_jaxpr/fg,...gzyx->...fzyx/dot_general | solution.py:69
  271.1 2.9 dynamic-slice_bitcast_fusion.17
  274.9 4.4 %multiply_subtract_fusion.17 = f32[35,8,32,33]{0,3,2,1:T(8,128)} fusion(f32[35,8,32,1]{0,3,2,1:T(1,128)S(1)} %get-tuple-element.546, f32[35,8,32,32]{0,3,2,1:T(8,128)S(1)} %dynamic-slice_bitcast_fusion.17, f32[35,8,32,1]{0,3,2,1:T(1,128)S(1)} %get-tuple-element.547, f32[35]{0:T(128)S(1)} %get-tuple-element.652, f32[]{:T(128)} %bitcast.150), kind=kLoop, calls=%fused_computation.32.clone.1 | loop fusion | flops 2365440 | bytes 2401424 | tf_op jit(solution)/shard_map/while/body/eval_jaxpr/sub | solution.py:50
  279.4 3.3 multiply_subtract_fusion.16
  283.3 4.1 %multiply_subtract_fusion.15 = f32[35,9,32,32]{0,3,2,1:T(8,128)} fusion(f32[35,10,32,32]{0,3,2,1:T(8,128)S(1)} %dynamic-slice_bitcast_fusion.16, f32[35]{0:T(128)S(1)} %get-tuple-element.652, f32[]{:T(128)} %bitcast.148), kind=kLoop, calls=%fused_computation.33.clone.1 | loop fusion | flops 1935360 | bytes 3870864 | tf_op jit(solution)/shard_map/while/body/eval_jaxpr/sub | solution.py:50
  289.9 3.2 copy.81
  293.2 14.1 %fusion.86 = f32[2,35,8,32,32]{1,4,3,2,0:T(8,128)} fusion(f32[2,35,8,32,32]{1,4,3,2,0:T(8,128)} %get-tuple-element.632, s32[]{:T(128)} %get-tuple-element.631, f32[35,9,32,32]{0,3,2,1:T(8,128)} %multiply_subtract_fusion.15, f32[35,8,33,32]{0,3,2,1:T(8,128)} %multiply_subtract_fusion.16, f32[35,8,32,33]{0,3,2,1:T(8,128)} %multiply_subtract_fusion.17, ...), kind=kOutput, calls=%fused_computation.41.clone.1 | convolution fusion | flops 122429440 | bytes 33593124 | tf_op jit(solution)/shard_map/while/body/eval_jaxpr/fg,...gzyx->...fzyx/dot_general | solution.py:69
  311.8 13.4 %multiply_add_fusion.1 = f32[2,35,8,32,32]{1,4,3,2,0:T(8,128)} fusion(f32[2,35,8,32,32]{1,4,3,2,0:T(8,128)} %get-tuple-element.589, f32[2,35,8,32,32]{1,4,3,2,0:T(8,128)} %get-tuple-element.152, f32[2,35,8,32,32]{1,4,3,2,0:T(8,128)} %get-tuple-element.153), kind=kLoop, calls=%fused_computation.80 | loop fusion | flops 1720320 | bytes 9175040 | tf_op jit(solution)/shard_map/add | solution.py:169
  325.3 7.2 %copy.61 = f32[2,35,8192]{2,0,1:T(2,128)} copy(f32[2,35,8192]{1,2,0:T(8,128)} %bitcast.167) | data formatting | bytes 4587520 | tf_op jit(solution)/shard_map/reshape | solution.py:177
  332.5 48.4 %all-reduce.3.cloned.1.call-done = f32[8,35,256]{2,0,1:T(8,128)} async-done(((f32[8,35,256]{2,0,1:T(8,128)}), f32[8,35,256]{2,0,1:T(8,128)}) %all-reduce.3.cloned.1.call-update) | async-done | bytes 286736
  (163 shorter events, 61.0 us)
Async XLA Ops:
  7.2 373.7 %all-reduce.3.cloned.1.call-start = ((), (), s32[]{:S(2)}) async-start(), calls=%async_computation | async-start | bytes 573440
  7.2 27.5 %copy-start.8 = (s32[2]{0:T(128)}, s32[2]{0:T(128)S(1)}, u32[]{:S(2)}) copy-start(s32[2]{0:T(128)S(1)} %iota_add_fusion.1) | copy-start | bytes 28
  36.3 11.1 %collective-permute-start = (bf16[2,35,1,16,16]{1,4,3,2,0:T(8,128)(2,1)S(1)}, bf16[2,35,1,16,16]{1,4,3,2,0:T(8,128)(2,1)S(1)}, u32[]{:S(2)}, u32[]{:S(2)}) collective-permute-start(bf16[2,35,1,16,16]{1,4,3,2,0:T(8,128)(2,1)S(1)} %get-tuple-element.340), channel_id=1, source_target_pairs={{0,1},{1,2},{2,3},{4,5},{5,6},{6,7},{8,9},{9,10},{10,11},{12,13},{... | collective-permute-start | bytes 107528 | tf_op jit(solution)/shard_map/ppermute | solution.py:19
  45.5 6.3 %collective-permute-start.1 = (bf16[2,35,1,16,16]{1,4,3,2,0:T(8,128)(2,1)S(1)}, bf16[2,35,1,16,16]{1,4,3,2,0:T(8,128)(2,1)S(1)}, u32[]{:S(2)}, u32[]{:S(2)}) collective-permute-start(bf16[2,35,1,16,16]{1,4,3,2,0:T(8,128)(2,1)S(1)} %get-tuple-element.341), channel_id=1, source_target_pairs={{1,0},{2,1},{3,2},{5,4},{6,5},{7,6},{9,8},{10,9},{11,10},{13,12},{... | collective-permute-start | bytes 107528 | tf_op jit(solution)/shard_map/ppermute | solution.py:22
  52.3 4.5 %copy-start.5 = (f32[2]{0:T(128)S(1)}, f32[2]{0:T(128)}, u32[]{:S(2)}) copy-start(f32[2]{0:T(128)} %constant.89.clone..sunk.2) | copy-start | bytes 28
  78.5 2.0 copy-start.1
  80.5 8.0 %collective-permute-start.2 = (bf16[2,35,1,32,32]{1,4,3,2,0:T(8,128)(2,1)S(1)}, bf16[2,35,1,32,32]{1,4,3,2,0:T(8,128)(2,1)S(1)}, u32[]{:S(2)}, u32[]{:S(2)}) collective-permute-start(bf16[2,35,1,32,32]{1,4,3,2,0:T(8,128)(2,1)S(1)} %get-tuple-element.338), channel_id=1, source_target_pairs={{0,1},{1,2},{2,3},{4,5},{5,6},{6,7},{8,9},{9,10},{10,11},{12,13},{... | collective-permute-start | bytes 430088 | tf_op jit(solution)/shard_map/ppermute | solution.py:19
  82.5 10.5 %collective-permute-start.3 = (bf16[2,35,1,32,32]{1,4,3,2,0:T(8,128)(2,1)S(1)}, bf16[2,35,1,32,32]{1,4,3,2,0:T(8,128)(2,1)S(1)}, u32[]{:S(2)}, u32[]{:S(2)}) collective-permute-start(bf16[2,35,1,32,32]{1,4,3,2,0:T(8,128)(2,1)S(1)} %get-tuple-element.339), channel_id=1, source_target_pairs={{1,0},{2,1},{3,2},{5,4},{6,5},{7,6},{9,8},{10,9},{11,10},{13,12},{... | collective-permute-start | bytes 430088 | tf_op jit(solution)/shard_map/ppermute | solution.py:22
  104.1 4.5 %copy-start.2 = (f32[35,35]{1,0:T(8,128)S(1)}, f32[35,35]{1,0:T(8,128)}, u32[]{:S(2)}) copy-start(f32[35,35]{1,0:T(8,128)} %param.18) | copy-start | bytes 14704
  104.1 4.5 %copy-start.3 = (f32[35]{0:T(128)S(1)}, f32[35]{0:T(128)}, u32[]{:S(2)}) copy-start(f32[35]{0:T(128)} %param.17) | copy-start | bytes 424
  104.1 4.5 %copy-start.4 = (f32[3]{0:T(128)S(1)}, f32[3]{0:T(128)}, u32[]{:S(2)}) copy-start(f32[3]{0:T(128)} %param.16) | copy-start | bytes 40
  112.7 7.9 %slice-start.5 = ((s8[10485760]{0:T(1024)(128)(4,1)}), s8[4194304]{0:T(1024)(128)(4,1)S(1)}, s32[]{:S(2)}) async-start(s8[10485760]{0:T(1024)(128)(4,1)} %bitcast.163), calls=%async_computation.6 | async-start | bytes 8388608 | tf_op jit(solution)/shard_map/while
  112.7 7.9 %slice-start.6 = ((s8[10485760]{0:T(1024)(128)(4,1)}), s8[4194304]{0:T(1024)(128)(4,1)S(1)}, s32[]{:S(2)}) async-start(s8[10485760]{0:T(1024)(128)(4,1)} %bitcast.163), calls=%async_computation.7 | async-start | bytes 8388608 | tf_op jit(solution)/shard_map/while
  117.1 3.4 slice-start.7
  153.4 7.9 %slice-start.5 = ((s8[10485760]{0:T(1024)(128)(4,1)}), s8[4194304]{0:T(1024)(128)(4,1)S(1)}, s32[]{:S(2)}) async-start(s8[10485760]{0:T(1024)(128)(4,1)} %bitcast.163), calls=%async_computation.6 | async-start | bytes 8388608 | tf_op jit(solution)/shard_map/while
  153.4 7.9 %slice-start.6 = ((s8[10485760]{0:T(1024)(128)(4,1)}), s8[4194304]{0:T(1024)(128)(4,1)S(1)}, s32[]{:S(2)}) async-start(s8[10485760]{0:T(1024)(128)(4,1)} %bitcast.163), calls=%async_computation.7 | async-start | bytes 8388608 | tf_op jit(solution)/shard_map/while
  157.8 3.4 slice-start.7
  190.2 19.4 %copy-start.10 = (u32[32]{0:T(128)S(1)}, u32[32]{0:T(128)}, u32[]{:S(2)}) copy-start(u32[32]{0:T(128)} %constant.94) | copy-start | bytes 388
  205.2 8.3 %collective-permute-start.4 = (bf16[2,35,1,32,32]{1,4,3,2,0:T(8,128)(2,1)}, bf16[2,35,1,32,32]{1,4,3,2,0:T(8,128)(2,1)S(1)}, u32[]{:S(2)}, u32[]{:S(2)}) collective-permute-start(bf16[2,35,1,32,32]{1,4,3,2,0:T(8,128)(2,1)} %get-tuple-element.336), channel_id=1, source_target_pairs={{0,1},{1,2},{2,3},{4,5},{5,6},{6,7},{8,9},{9,10},{10,11},{12,13},{... | collective-permute-start | bytes 430088 | tf_op jit(solution)/shard_map/ppermute | solution.py:19
  207.2 10.5 %collective-permute-start.5 = (bf16[2,35,1,32,32]{1,4,3,2,0:T(8,128)(2,1)S(1)}, bf16[2,35,1,32,32]{1,4,3,2,0:T(8,128)(2,1)S(1)}, u32[]{:S(2)}, u32[]{:S(2)}) collective-permute-start(bf16[2,35,1,32,32]{1,4,3,2,0:T(8,128)(2,1)S(1)} %get-tuple-element.337), channel_id=1, source_target_pairs={{1,0},{2,1},{3,2},{5,4},{6,5},{7,6},{9,8},{10,9},{11,10},{13,12},{... | collective-permute-start | bytes 430088 | tf_op jit(solution)/shard_map/ppermute | solution.py:22
  217.7 4.0 %copy-start = (f32[2,35,8,32,32]{1,4,3,2,0:T(8,128)S(1)}, f32[2,35,8,32,32]{1,4,3,2,0:T(8,128)}, u32[]{:S(2)}) copy-start(f32[2,35,8,32,32]{1,4,3,2,0:T(8,128)} %get-tuple-element.625) | copy-start | bytes 6881284
  236.0 7.8 %slice-start.2 = ((s8[10485760]{0:T(1024)(128)(4,1)}), s8[4194304]{0:T(1024)(128)(4,1)S(1)}, s32[]{:S(2)}) async-start(s8[10485760]{0:T(1024)(128)(4,1)} %bitcast.161), calls=%async_computation.3 | async-start | bytes 8388608 | tf_op jit(solution)/shard_map/while
  236.0 7.8 %slice-start.3 = ((s8[10485760]{0:T(1024)(128)(4,1)}), s8[4194304]{0:T(1024)(128)(4,1)S(1)}, s32[]{:S(2)}) async-start(s8[10485760]{0:T(1024)(128)(4,1)} %bitcast.161), calls=%async_computation.4 | async-start | bytes 8388608 | tf_op jit(solution)/shard_map/while
  240.5 3.4 slice-start.4
  243.8 4.7 %slice-start = ((s8[8388608]{0:T(1024)(128)(4,1)}), s8[4194304]{0:T(1024)(128)(4,1)S(1)}, s32[]{:S(2)}) async-start(s8[8388608]{0:T(1024)(128)(4,1)} %bitcast.158), calls=%async_computation.1 | async-start | bytes 8388608 | tf_op jit(solution)/shard_map/while
  244.4 4.1 %slice-start.1 = ((s8[8388608]{0:T(1024)(128)(4,1)}), s8[4194304]{0:T(1024)(128)(4,1)S(1)}, s32[]{:S(2)}) async-start(s8[8388608]{0:T(1024)(128)(4,1)} %bitcast.158), calls=%async_computation.2 | async-start | bytes 8388608 | tf_op jit(solution)/shard_map/while
  274.9 7.8 %slice-start.2 = ((s8[10485760]{0:T(1024)(128)(4,1)}), s8[4194304]{0:T(1024)(128)(4,1)S(1)}, s32[]{:S(2)}) async-start(s8[10485760]{0:T(1024)(128)(4,1)} %bitcast.161), calls=%async_computation.3 | async-start | bytes 8388608 | tf_op jit(solution)/shard_map/while
  274.9 7.8 %slice-start.3 = ((s8[10485760]{0:T(1024)(128)(4,1)}), s8[4194304]{0:T(1024)(128)(4,1)S(1)}, s32[]{:S(2)}) async-start(s8[10485760]{0:T(1024)(128)(4,1)} %bitcast.161), calls=%async_computation.4 | async-start | bytes 8388608 | tf_op jit(solution)/shard_map/while
  279.4 3.4 slice-start.4
  282.7 4.7 %slice-start = ((s8[8388608]{0:T(1024)(128)(4,1)}), s8[4194304]{0:T(1024)(128)(4,1)S(1)}, s32[]{:S(2)}) async-start(s8[8388608]{0:T(1024)(128)(4,1)} %bitcast.158), calls=%async_computation.1 | async-start | bytes 8388608 | tf_op jit(solution)/shard_map/while
  283.3 4.1 %slice-start.1 = ((s8[8388608]{0:T(1024)(128)(4,1)}), s8[4194304]{0:T(1024)(128)(4,1)S(1)}, s32[]{:S(2)}) async-start(s8[8388608]{0:T(1024)(128)(4,1)} %bitcast.158), calls=%async_computation.2 | async-start | bytes 8388608 | tf_op jit(solution)/shard_map/while
  310.0 0.7 copy-start.7
  310.0 0.7 copy-start.9
  325.3 55.6 %copy-start.6 = (f32[1,35,256]{2,0,1:T(1,128)S(1)}, f32[1,35,256]{2,0,1:T(1,128)}, u32[]{:S(2)}) copy-start(f32[1,35,256]{2,0,1:T(1,128)} %param.14) | copy-start | bytes 107524
Sparse Core Ops, SparseCore 0:
  312.0 68.8 all-reduce.2
where the time goes:
time: 394 us; the launch traced here: 390 us
  other arithmetic  110 us (28%)
  local copies, waits for them, and re-layouts  90.3 us (23%)
  waiting for transfers between devices  68.1 us (17%)
  matrix products  58.5 us (15%)
  blocking collectives  27.5 us (7%)
  starting transfers between devices  19.8 us (5%)
  between operations  14.4 us (4%)
    dot_general x4, matrix products, tendency(): jnp.einsum('fg,...gzyx->...fzyx', stoich, reaction_rate, precision=highest)  56.3 us
    unnamed x2, waiting for transfers between devices  48.4 us
    sub x12, other arithmetic, face_flux(): speed * (left_side + right_side) * 0.5 - diffuse * (right_side - left_side)  46.7 us
    all_gather x1, blocking collectives, shards(): lax.all_gather(coarse_send, 'gx', axis=0, tiled=True)  27.5 us
    convert_element_type x2, other arithmetic, extend_layers(): cells.astype(jnp.bfloat16)  17.4 us
    concatenate x2, other arithmetic, extend_layers(): return jnp.concatenate([lower_ghost, cells, upper_ghost], 2)  15.1 us
    squeeze x8, local copies, waits for them, and re-layouts, tendency_slots(): return lax.map(tendency_one_slot, (padded_layers, cells))  14.1 us
    slice x4, local copies, waits for them, and re-layouts, tendency(): reaction_rate = cells * jax.nn.sigmoid(heat_gain * cells[..., 0:1, :, :, :])  14.1 us
  transfers between devices with their start and end apart: 7, of which 6 were waited for; matrix products, arithmetic and copies ran while one was open for 5% of the time, Pallas kernels for 0%

commit v1 on v0

v1 whole, which is shorter than its diff:
```python
import functools

import jax
import jax.numpy as jnp
import numpy as np
from jax import lax
from jax.experimental import pallas as pl
from jax.experimental.pallas import tpu as pltpu
from jax.sharding import PartitionSpec as P

CB = 16
FINE = 2 * CB
CELLS = CB * CB
AREA = FINE * FINE
TILE = 128
ROWS = 40
PAD = 48
DIRECT = 8

time_step = 0.25
heat_gain = 2.0


def interpolation():
    slope = np.zeros((CB, CB), np.float32)
    for i in range(1, CB - 1):
        slope[i + 1, i], slope[i - 1, i] = 0.5, -0.5
    slope[1, 0], slope[0, 0] = 1.0, -1.0
    slope[-1, -1], slope[-2, -1] = 1.0, -1.0
    copy = np.zeros((CB, FINE), np.float32)
    tilt = np.zeros((CB, FINE), np.float32)
    for i in range(CB):
        for a in range(2):
            copy[i, 2 * i + a] = 1.0
            tilt[:, 2 * i + a] = slope[:, i] * (a - 0.5) * 0.5
    same = np.kron(copy, copy)
    full = same + np.kron(copy, tilt) + np.kron(tilt, copy)
    return full, same


def strips():
    edge = np.arange(FINE)
    last = FINE - 1
    border = [edge * FINE, edge * FINE + last, edge, last * FINE + edge]
    inner = [edge * FINE + 1, edge * FINE + last - 1, FINE + edge, (last - 1) * FINE + edge]
    return np.concatenate(border), np.concatenate(inner)


def pair_sums(layers):
    place = np.zeros((layers * TILE, layers * TILE // 2), np.float32)
    for k in range(layers):
        for lane in range(TILE):
            place[k * TILE + lane, k * TILE // 2 + lane // 2] = 0.25
    return place


def fill_coarse(stack, own, low, high, layers):
    fields = own.shape[1]
    stack[...] = jnp.zeros_like(stack)
    for k in range(layers + 4):
        if k < 2:
            source, at = low, k
        elif k < layers + 2:
            source, at = own, k - 2
        else:
            source, at = high, k - layers - 2
        stack[k * PAD : k * PAD + fields, :] = source[0, :, at * CELLS : (at + 1) * CELLS]


def edge_ghosts(parts, bottom, top, layers, width):
    def rows(k):
        return slice((k + 2) * PAD, (k + 2) * PAD + ROWS)

    @pl.when(bottom)
    def _():
        parts[rows(-1), width:] = 2.0 * parts[rows(0), width:] - parts[rows(1), width:]

    @pl.when(top)
    def _():
        parts[rows(layers), width:] = (
            2.0 * parts[rows(layers - 1), width:] - parts[rows(layers - 2), width:]
        )


def fine_layers(start, parts, layers, width):
    step = 2 * TILE

    def rows(k):
        return pl.ds(pl.multiple_of((k + 1) * PAD, 16), ROWS)

    def body(k, carry):
        for c in range(0, width, step):
            lanes = slice(c, c + step)
            copies = slice(width + c, width + c + step)
            centre = parts[rows(k), lanes]
            tilt = (parts[rows(k + 1), copies] - parts[rows(k - 1), copies]) * 0.125
            start[2 * k, :, lanes] = centre - tilt
            start[2 * k + 1, :, lanes] = centre + tilt
        return carry

    lax.fori_loop(0, layers + 2, body, 0)


def split_coupling(coupling):
    value = coupling[...]
    head = value.astype(jnp.bfloat16)
    rest = (value - head.astype(jnp.float32)).astype(jnp.bfloat16)
    column = lax.broadcasted_iota(jnp.int32, value.shape, 1)
    return jnp.where(column < 2 * PAD, head.astype(jnp.float32), rest.astype(jnp.float32)).astype(
        jnp.bfloat16
    )


def store_rate(rate, lanes, cells, warm):
    value = cells * warm
    head = value.astype(jnp.bfloat16)
    rest = (value - head.astype(jnp.float32)).astype(jnp.bfloat16)
    rate[0:ROWS, lanes] = head
    rate[PAD : PAD + ROWS, lanes] = rest
    rate[2 * PAD : 2 * PAD + ROWS, lanes] = head


def sources(rate, mixed):
    return jnp.dot(mixed, rate[...], preferred_element_type=jnp.float32)


def stage(field, z, rate, mixed, velocity, diffuse, emit):
    count = AREA // TILE
    lane = lax.broadcasted_iota(jnp.int32, (ROWS, TILE), 1)
    pos = lane % FINE
    at_low, at_high = pos == 0, pos == FINE - 1
    head, tail = lane < FINE, lane >= TILE - FINE
    half = [velocity[d] * 0.5 for d in range(3)]
    warm = jax.nn.sigmoid(heat_gain * field[z, 0:1, :])
    for t in range(count):
        lanes = slice(t * TILE, (t + 1) * TILE)
        store_rate(rate, lanes, field[z, :, lanes], warm[:, lanes])
    source = sources(rate, mixed)
    tiles = {}
    ups = {}
    downs = {}

    def tile(t):
        if t not in tiles:
            tiles[t] = field[z, :, t * TILE : (t + 1) * TILE]
            ups[t] = pltpu.roll(tiles[t], TILE - FINE, 1)
            downs[t] = pltpu.roll(tiles[t], FINE, 1)
        return tiles[t]

    for t in range(count):
        lanes = slice(t * TILE, (t + 1) * TILE)
        cells = tile(t)
        x_low = jnp.where(at_low, cells, pltpu.roll(cells, 1, 1))
        x_high = jnp.where(at_high, cells, pltpu.roll(cells, TILE - 1, 1))
        if t + 1 < count:
            tile(t + 1)
        y_low = jnp.where(head, downs[t - 1] if t else cells, downs[t])
        y_high = jnp.where(tail, ups[t + 1] if t + 1 < count else cells, ups[t])
        z_low = field[z - 1, :, lanes]
        z_high = field[z + 1, :, lanes]
        drift = (
            half[0] * (x_high - x_low) + half[1] * (y_high - y_low) + half[2] * (z_high - z_low)
        )
        spread = (x_high + x_low) + (y_high + y_low) + (z_high + z_low) - 6.0 * cells
        emit(lanes, cells, source[:, lanes] - drift + diffuse * spread)


def step_kernel(
    layers,
    flags,
    velocity,
    own,
    low,
    high,
    weights,
    coupling,
    diffusivity,
    out,
    stack,
    parts,
    start,
    middle,
    rate,
):
    bottom, top = flags[0] == 1, flags[1] == 1
    fields = own.shape[1]
    depth = 2 * layers
    rate[...] = jnp.zeros_like(rate)
    fill_coarse(stack, own, low, high, layers)
    parts[...] = jnp.dot(stack[...], weights[...], preferred_element_type=jnp.float32)
    edge_ghosts(parts, bottom, top, layers, AREA)
    fine_layers(start, parts, layers, AREA)

    @pl.when(bottom)
    def _():
        start[1] = start[2]

    @pl.when(top)
    def _():
        start[depth + 2] = start[depth + 1]

    mixed = split_coupling(coupling)
    diffuse = jnp.broadcast_to(diffusivity[...], (ROWS, TILE))

    def first(i, carry):
        def emit(lanes, cells, change):
            middle[i, :, lanes] = cells + time_step * change

        stage(start, i + 1, rate, mixed, velocity, diffuse, emit)
        return carry

    lax.fori_loop(0, depth + 2, first, 0)

    @pl.when(bottom)
    def _():
        middle[0] = middle[1]

    @pl.when(top)
    def _():
        middle[depth + 1] = middle[depth]

    def second(i, carry):
        def emit(lanes, cells, change):
            value = (start[i + 2, :, lanes] + cells) * 0.5 + (time_step * 0.5) * change
            at = pl.multiple_of(i * AREA + lanes.start, TILE)
            out[0, :, pl.ds(at, TILE)] = value[:fields]

        stage(middle, i + 1, rate, mixed, velocity, diffuse, emit)
        return carry

    lax.fori_loop(0, depth, second, 0)


def side_kernel(
    layers,
    flags,
    velocity,
    own,
    low,
    high,
    weights,
    coupling,
    diffusivity,
    place,
    fluxes,
    out,
    stack,
    parts,
    start,
    rate,
    faces,
):
    bottom, top = flags[0] == 1, flags[1] == 1
    fields = own.shape[1]
    depth = 2 * layers
    width = 2 * TILE
    rate[...] = jnp.zeros_like(rate)
    fill_coarse(stack, own, low, high, layers)
    parts[...] = jnp.dot(stack[...], weights[...], preferred_element_type=jnp.float32)
    edge_ghosts(parts, bottom, top, layers, width)
    fine_layers(start, parts, layers, width)

    @pl.when(bottom)
    def _():
        start[1] = start[2]

    @pl.when(top)
    def _():
        start[depth + 2] = start[depth + 1]

    mixed = split_coupling(coupling)
    diffuse = jnp.broadcast_to(diffusivity[...], (ROWS, TILE))
    lane = lax.broadcasted_iota(jnp.int32, (ROWS, TILE), 1)
    pos = lane % FINE
    side = lane // FINE
    at_low, at_high = pos == 0, pos == FINE - 1
    normal = jnp.where(side < 2, velocity[0], velocity[1])
    along = jnp.where(side < 2, velocity[1], velocity[0]) * 0.5
    inward = jnp.where(side % 2 == 0, normal, -normal) * 0.5
    half_z = velocity[2] * 0.5
    border = slice(0, TILE)
    inner = slice(TILE, 2 * TILE)
    for i in range(depth):
        warm = jax.nn.sigmoid(heat_gain * start[i + 2, 0:1, border])
        store_rate(rate, slice(i * TILE, (i + 1) * TILE), start[i + 2, :, border], warm)
    source = sources(rate, mixed)
    totals = []
    for i in range(depth):
        cells = start[i + 2, :, border]
        gap = start[i + 2, :, inner] - cells
        behind = jnp.where(at_low, cells, pltpu.roll(cells, 1, 1))
        ahead = jnp.where(at_high, cells, pltpu.roll(cells, TILE - 1, 1))
        z_low = start[i + 1, :, border]
        z_high = start[i + 3, :, border]
        drift = inward * gap + along * (ahead - behind) + half_z * (z_high - z_low)
        spread = gap + (ahead + behind) + (z_high + z_low) - 4.0 * cells
        change = source[:, i * TILE : (i + 1) * TILE] - drift + diffuse * spread
        later = cells + time_step * change
        totals.append((normal * cells + normal * later) * 0.5)
    for k in range(layers):
        faces[:, k * TILE : (k + 1) * TILE] = totals[2 * k] + totals[2 * k + 1]
    summed = jnp.dot(
        faces[...],
        place[...],
        precision=lax.Precision.HIGHEST,
        preferred_element_type=jnp.float32,
    )
    out[0] = summed[:fields] - fluxes[0]


def whole(shape):
    return pl.BlockSpec(shape, lambda s: (0,) * len(shape))


def per_slot(shape):
    return pl.BlockSpec((1,) + shape, lambda s: (s,) + (0,) * len(shape))


def scalars():
    return pl.BlockSpec(memory_space=pltpu.SMEM)


def fine_step(flags, velocity, own, low, high, coupling, diffusivity):
    slots, fields, cells = own.shape
    layers = cells // CELLS
    full, same = interpolation()
    weights = jnp.asarray(np.concatenate([full, same], 1), jnp.bfloat16)
    return pl.pallas_call(
        functools.partial(step_kernel, layers),
        grid=(slots,),
        in_specs=[
            scalars(),
            scalars(),
            per_slot((fields, cells)),
            per_slot((fields, 2 * CELLS)),
            per_slot((fields, 2 * CELLS)),
            whole(weights.shape),
            whole(coupling.shape),
            whole(diffusivity.shape),
        ],
        out_specs=per_slot((fields, 2 * layers * AREA)),
        out_shape=jax.ShapeDtypeStruct((slots, fields, 2 * layers * AREA), jnp.float32),
        scratch_shapes=[
            pltpu.VMEM(((layers + 4) * PAD, CELLS), jnp.bfloat16),
            pltpu.VMEM(((layers + 4) * PAD, 2 * AREA), jnp.float32),
            pltpu.VMEM((2 * layers + 4, ROWS, AREA), jnp.float32),
            pltpu.VMEM((2 * layers + 2, ROWS, AREA), jnp.float32),
            pltpu.VMEM((3 * PAD, AREA), jnp.bfloat16),
        ],
        cost_estimate=pl.CostEstimate(
            flops=slots * 2000000000, bytes_accessed=8000000, transcendentals=0
        ),
        name="fine_step",
    )(flags, velocity, own, low, high, weights, coupling, diffusivity)


def side_fluxes(flags, velocity, own, low, high, coupling, diffusivity, fluxes):
    slots, fields, cells = own.shape
    layers = cells // CELLS
    full, same = interpolation()
    border, inner = strips()
    picked = np.concatenate([border, inner])
    weights = jnp.asarray(np.concatenate([full[:, picked], same[:, picked]], 1), jnp.bfloat16)
    place = jnp.asarray(pair_sums(layers))
    return pl.pallas_call(
        functools.partial(side_kernel, layers),
        grid=(slots,),
        in_specs=[
            scalars(),
            scalars(),
            per_slot((fields, cells)),
            per_slot((fields, 2 * CELLS)),
            per_slot((fields, 2 * CELLS)),
            whole(weights.shape),
            whole(coupling.shape),
            whole(diffusivity.shape),
            whole(place.shape),
            per_slot(fluxes.shape[1:]),
        ],
        out_specs=per_slot(fluxes.shape[1:]),
        out_shape=jax.ShapeDtypeStruct(fluxes.shape, jnp.float32),
        scratch_shapes=[
            pltpu.VMEM(((layers + 4) * PAD, CELLS), jnp.bfloat16),
            pltpu.VMEM(((layers + 4) * PAD, 4 * TILE), jnp.float32),
            pltpu.VMEM((2 * layers + 4, ROWS, 2 * TILE), jnp.float32),
            pltpu.VMEM((3 * PAD, 2 * layers * TILE), jnp.bfloat16),
            pltpu.VMEM((ROWS, layers * TILE), jnp.float32),
        ],
        cost_estimate=pl.CostEstimate(
            flops=slots * 400000000, bytes_accessed=2000000, transcendentals=0
        ),
        name="side_fluxes",
    )(flags, velocity, own, low, high, weights, coupling, diffusivity, place, fluxes)


def halo(block):
    count = lax.axis_size("gy")
    forward = [(i, i + 1) for i in range(count - 1)]
    backward = [(i + 1, i) for i in range(count - 1)]
    low = lax.ppermute(block[:, :, -2 * CELLS :], "gy", forward)
    high = lax.ppermute(block[:, :, : 2 * CELLS], "gy", backward)
    return low, high


def fetch(coarse, patch_owner, my_slots):
    groups = lax.axis_size("gx")
    group = lax.axis_index("gx")
    send_slots = coarse.shape[0]
    if groups > DIRECT:
        chooser = (my_slots[:, None] == patch_owner[None, :]).astype(coarse.dtype)
        everything = lax.all_gather(coarse, "gx", axis=0, tiled=True)
        return jnp.einsum("oq,qfc->ofc", chooser, everything)
    blocks = [coarse] + [
        lax.ppermute(coarse, "gx", [(i, (i + shift) % groups) for i in range(groups)])
        for shift in range(1, groups)
    ]
    picked = []
    for s in range(my_slots.shape[0]):
        value = jnp.zeros_like(coarse[0])
        for shift in range(groups):
            origin = lax.rem(group - shift + groups, groups)
            for t in range(send_slots):
                owner = lax.dynamic_index_in_dim(
                    patch_owner, origin * send_slots + t, 0, keepdims=False
                )
                value = jnp.where(owner == my_slots[s], blocks[shift][t], value)
        picked.append(value)
    return jnp.stack(picked)


def shards(coarse_send, coarse_flux, patch_owner, velocity, diffusivity, stoich):
    send_slots, fields, _ = coarse_send.shape
    own_slots = 2 * send_slots
    pencil = lax.axis_index("gy")
    pencils = lax.axis_size("gy")
    my_slots = lax.axis_index("gx") * own_slots + jnp.arange(own_slots, dtype=jnp.int32)
    flags = jnp.stack([pencil == 0, pencil == pencils - 1]).astype(jnp.int32)
    square = jnp.pad(stoich, ((0, ROWS - fields), (0, PAD - fields)))
    coupling = jnp.concatenate([square, square, square], 1)
    diffuse = jnp.pad(diffusivity, (0, ROWS - fields)).reshape(ROWS, 1)
    low, high = halo(coarse_send)
    coarse = fetch(coarse_send, patch_owner, my_slots)
    reflux = side_fluxes(
        flags, velocity, coarse_send, low, high, coupling, diffuse, coarse_flux
    )
    slot_low, slot_high = halo(coarse)
    fine_state = fine_step(
        flags, velocity, coarse, slot_low, slot_high, coupling, diffuse
    )
    return fine_state, reflux


def solution(mesh):
    placed = (P("gx", None, "gy"), P("gx", None, "gy"), P(), P(), P(), P())
    return jax.shard_map(
        shards,
        mesh=mesh,
        in_specs=placed,
        out_specs=(P("gx", None, "gy"), P("gx", None, "gy")),
        check_vma=False,
    )
```

time: 394 us -> 77.9 us (0.20)
  other arithmetic: 110 us -> 2.17 us
  local copies, waits for them, and re-layouts: 90.3 us -> 12.9 us
  waiting for transfers between devices: 68.1 us -> 0.8 us
  matrix products: 58.5 us -> 0 us
  blocking collectives: 27.5 us -> 0 us
  Pallas kernels: 0 us -> 17.9 us
  between operations: 14.4 us -> 20.2 us
    dot_general x6 -> x0, matrix products: 58.5 us -> none  [the longest x4 56.3 us: tendency(): jnp.einsum('fg,...gzyx->...fzyx', stoich, reaction_rate, precision=highest)]
    sub x17 -> x0, other arithmetic: 49 us -> none  [the longest x12 46.7 us: face_flux(): speed * (left_side + right_side) * 0.5 - diffuse * (right_side - left_side)]
    unnamed x2 -> x0, waiting for transfers between devices: 48.4 us -> none
    all_gather x1 -> x0, blocking collectives: 27.5 us -> none  [shards(): lax.all_gather(coarse_send, 'gx', axis=0, tiled=True)]
    slice x23 -> x2, local copies, waits for them, and re-layouts: 26.7 us -> 2.44 us  [the longest x1 1.62 us: fetch(): value = jnp.where(owner == my_slots[s], blocks[shift][t], value)]
    add x6 -> x1, other arithmetic: 21.4 us -> 0.01 us  [shards(): lax.axis_index('gx') * own_slots + jnp.arange(own_slots, dtype=jnp.int32)]
    ppermute x6 -> x11, waiting for transfers between devices: 19.8 us -> 0.8 us  [the longest x2 0.77 us: halo(): low = lax.ppermute(block[:, :, -2 * CELLS:], 'gy', forward)]
    pallas_call x0 -> x2, Pallas kernels: none -> 17.9 us  [the longest x1 14.8 us: fine_step(): pl.pallas_call(functools.partial(step_kernel, layers), grid=(slots,), in_...]
  transfers between devices with their start and end apart: 7 -> 11, of which waited for: 6 -> 1; matrix products, arithmetic and copies ran while one was open for 5% -> 12% of each run, Pallas kernels for 0% -> 4%
where the time goes in v1:
time: 77.9 us; the launch traced here: 77.1 us
  starting transfers between devices  23.2 us (30%)
  between operations  20.2 us (26%)
  Pallas kernels  17.9 us (23%)
  local copies, waits for them, and re-layouts  12.9 us (17%)
  other arithmetic  2.17 us (3%)
  waiting for transfers between devices  0.8 us (1%)
    pallas_call x1, Pallas kernels, fine_step(): pl.pallas_call(functools.partial(step_kernel, layers), grid=(slots,), in_...  14.8 us
    ppermute x7, starting transfers between devices, fetch(): lax.ppermute(coarse, 'gx', [(i, (i + shift) % groups) for i in range(grou...  11.2 us
    unnamed x13, local copies, waits for them, and re-layouts  8.35 us
    ppermute x2, starting transfers between devices, halo(): low = lax.ppermute(block[:, :, -2 * CELLS:], 'gy', forward)  6.15 us
    ppermute x2, starting transfers between devices, halo(): high = lax.ppermute(block[:, :, :2 * CELLS], 'gy', backward)  5.84 us
    pallas_call x1, Pallas kernels, side_fluxes(): pl.pallas_call(functools.partial(side_kernel, layers), grid=(slots,), in_...  3.03 us
    slice x1, local copies, waits for them, and re-layouts, fetch(): value = jnp.where(owner == my_slots[s], blocks[shift][t], value)  1.62 us
  transfers between devices with their start and end apart: 11, of which 1 were waited for; matrix products, arithmetic and copies ran while one was open for 12% of the time, Pallas kernels for 4%

profile of v1, /device:TPU:1, one launch (start us, length us, event | category | flops | bytes accessed | tf_op | source)
XLA Modules:
  0.0 77.1 jit_solution(3754926852059973994)
XLA Ops:
  0.6 0.0 copy-start
  0.6 2.1 %collective-permute-start.6 = (bf16[1,35,1024]{2,1,0:T(8,128)(2,1)}, bf16[1,35,1024]{2,1,0:T(8,128)(2,1)S(1)}, u32[]{:S(2)}, u32[]{:S(2)}) collective-permute-start(bf16[1,35,1024]{2,1,0:T(8,128)(2,1)} %own.1), channel_id=1, source_target_pairs={{0,4},{4,8},{8,12},{12,16},{16,20},{20,24},{24,28},{28,0},{1,5},{5... | collective-permute-start | bytes 215048 | tf_op jit(solution)/shard_map/ppermute | solution.py:414
  2.8 1.3 %collective-permute-start.5 = (bf16[1,35,1024]{2,1,0:T(8,128)(2,1)}, bf16[1,35,1024]{2,1,0:T(8,128)(2,1)S(1)}, u32[]{:S(2)}, u32[]{:S(2)}) collective-permute-start(bf16[1,35,1024]{2,1,0:T(8,128)(2,1)} %own.1), channel_id=1, source_target_pairs={{0,8},{4,12},{8,16},{12,20},{16,24},{20,28},{24,0},{28,4},{1,9},{5... | collective-permute-start | bytes 215048 | tf_op jit(solution)/shard_map/ppermute | solution.py:414
  4.0 2.3 %collective-permute-start.4 = (bf16[1,35,1024]{2,1,0:T(8,128)(2,1)}, bf16[1,35,1024]{2,1,0:T(8,128)(2,1)S(1)}, u32[]{:S(2)}, u32[]{:S(2)}) collective-permute-start(bf16[1,35,1024]{2,1,0:T(8,128)(2,1)} %own.1), channel_id=1, source_target_pairs={{0,12},{4,16},{8,20},{12,24},{16,28},{20,0},{24,4},{28,8},{1,13},{... | collective-permute-start | bytes 215048 | tf_op jit(solution)/shard_map/ppermute | solution.py:414
  6.3 0.8 %fusion.2 = (bf16[1,35,512]{2,1,0:T(8,128)(2,1)S(1)}, bf16[1,35,512]{2,1,0:T(8,128)(2,1)S(1)}) fusion(bf16[1,35,1024]{2,1,0:T(8,128)(2,1)} %own.1), kind=kLoop, calls=%fused_computation.13 | loop fusion | bytes 143360 | tf_op jit(solution)/shard_map/slice | solution.py:401
  7.1 3.4 %collective-permute-start.10 = (bf16[1,35,512]{2,1,0:T(8,128)(2,1)S(1)}, bf16[1,35,512]{2,1,0:T(8,128)(2,1)S(1)}, u32[]{:S(2)}, u32[]{:S(2)}) collective-permute-start(bf16[1,35,512]{2,1,0:T(8,128)(2,1)S(1)} %get-tuple-element.6), channel_id=1, source_target_pairs={{1,0},{2,1},{3,2},{5,4},{6,5},{7,6},{9,8},{10,9},{11,10},{13,12},{... | collective-permute-start | bytes 107528 | tf_op jit(solution)/shard_map/ppermute | solution.py:401
  10.5 3.0 %collective-permute-start.9 = (bf16[1,35,512]{2,1,0:T(8,128)(2,1)S(1)}, bf16[1,35,512]{2,1,0:T(8,128)(2,1)S(1)}, u32[]{:S(2)}, u32[]{:S(2)}) collective-permute-start(bf16[1,35,512]{2,1,0:T(8,128)(2,1)S(1)} %get-tuple-element.7), channel_id=1, source_target_pairs={{0,1},{1,2},{2,3},{4,5},{5,6},{6,7},{8,9},{9,10},{10,11},{12,13},{... | collective-permute-start | bytes 107528 | tf_op jit(solution)/shard_map/ppermute | solution.py:400
  13.6 0.7 pad.8
  14.4 0.7 pad_maximum_fusion.1.coupling
  15.1 1.6 %fusion.3 = (s32[1]{0:T(128)}, s32[1]{0:T(128)}, s32[1]{0:T(128)}, s32[1]{0:T(128)}, s32[1]{0:T(128)}, /*index=5*/s32[1]{0:T(128)}, s32[1]{0:T(128)}, s32[1]{0:T(128)}, s32[1]{0:T(128)}, s32[1]{0:T(128)}) fusion(s32[2]{0:T(128)S(1)} %iota_add_fusion, s32[8]{0:T(128)} %param.11, s32[]{:T(128)S(6)} %select_n.159, s32[]{:T(128)S(6)} %select_n.161, ...), kind=kLoop, calls=%fused_computation.14 | loop fusion | bytes 112 | tf_op jit(solution)/shard_map/slice | solution.py:426
  16.7 0.7 pad_bitcast_fusion
  17.4 0.0 collective-permute-done.10.high
  17.4 0.0 copy-start.3
  17.4 1.0 %collective-permute-start.3 = (bf16[1,35,1024]{2,1,0:T(8,128)(2,1)}, bf16[1,35,1024]{2,1,0:T(8,128)(2,1)S(1)}, u32[]{:S(2)}, u32[]{:S(2)}) collective-permute-start(bf16[1,35,1024]{2,1,0:T(8,128)(2,1)} %own.1), channel_id=1, source_target_pairs={{0,16},{4,20},{8,24},{12,28},{16,0},{20,4},{24,8},{28,12},{1,17},{... | collective-permute-start | bytes 215048 | tf_op jit(solution)/shard_map/ppermute | solution.py:414
  18.3 0.0 collective-permute-done.9.low
  18.3 0.0 copy-start.4
  18.3 2.4 %collective-permute-start.2 = (bf16[1,35,1024]{2,1,0:T(8,128)(2,1)}, bf16[1,35,1024]{2,1,0:T(8,128)(2,1)S(1)}, u32[]{:S(2)}, u32[]{:S(2)}) collective-permute-start(bf16[1,35,1024]{2,1,0:T(8,128)(2,1)} %own.1), channel_id=1, source_target_pairs={{0,20},{4,24},{8,28},{12,0},{16,4},{20,8},{24,12},{28,16},{1,21},{... | collective-permute-start | bytes 215048 | tf_op jit(solution)/shard_map/ppermute | solution.py:414
  20.7 0.0 collective-permute-done.6
  20.7 1.1 %collective-permute-start.1 = (bf16[1,35,1024]{2,1,0:T(8,128)(2,1)}, bf16[1,35,1024]{2,1,0:T(8,128)(2,1)S(1)}, u32[]{:S(2)}, u32[]{:S(2)}) collective-permute-start(bf16[1,35,1024]{2,1,0:T(8,128)(2,1)} %own.1), channel_id=1, source_target_pairs={{0,24},{4,28},{8,0},{12,4},{16,8},{20,12},{24,16},{28,20},{1,25},{... | collective-permute-start | bytes 215048 | tf_op jit(solution)/shard_map/ppermute | solution.py:414
  21.8 0.0 collective-permute-done.5
  21.8 1.1 %collective-permute-start = (bf16[1,35,1024]{2,1,0:T(8,128)(2,1)}, bf16[1,35,1024]{2,1,0:T(8,128)(2,1)S(1)}, u32[]{:S(2)}, u32[]{:S(2)}) collective-permute-start(bf16[1,35,1024]{2,1,0:T(8,128)(2,1)} %own.1), channel_id=1, source_target_pairs={{0,28},{4,0},{8,4},{12,8},{16,12},{20,16},{24,20},{28,24},{1,29},{... | collective-permute-start | bytes 215048 | tf_op jit(solution)/shard_map/ppermute | solution.py:414
  22.9 0.7 add_convert_fusion.flags
  43.0 0.7 copy.11.diffusivity
  43.7 1.4 %copy.13.fluxes = f32[1,35,256]{2,1,0:T(8,128)} copy(f32[1,35,256]{2,0,1:T(1,128)} %param.10) | data formatting | bytes 71680 | tf_op args[1]
  45.0 0.0 copy-done.3
  45.1 0.0 copy-done.4
  45.1 3.0 %side_fluxes.1 = f32[1,35,256]{2,1,0:T(8,128)} custom-call(s32[2]{0:T(128)} %add_convert_fusion.flags, f32[3]{0:T(128)} %velocity.3, bf16[1,35,1024]{2,1,0:T(8,128)(2,1)} %own.1, bf16[1,35,512]{2,1,0:T(8,128)(2,1)} %copy-done.4, bf16[1,35,512]{2,1,0:T(8,128)(2,1)} %copy-done.3, bf16[256,512]{1,0:T(8,128)(2,1)} %constant.101.clone.weights, ...), custom_call_target="tpu_custom_call" | custom-call | flops 400000000 | bytes 2000000 | tf_op jit(solution)/shard_map/side_fluxes/pallas_call | solution.py:365
  48.1 1.4 %copy.15 = f32[1,35,256]{2,0,1:T(1,128)} copy(f32[1,35,256]{2,1,0:T(8,128)} %side_fluxes.1) | data formatting | bytes 71680
  49.5 0.0 collective-permute-done.4
  49.5 0.0 collective-permute-done.3
  49.5 0.0 collective-permute-done.2
  49.5 0.0 collective-permute-done.1
  49.5 0.0 collective-permute-done
  49.6 0.0 copy-done
  49.7 2.4 %collective-permute-start.8 = (bf16[2,35,512]{2,1,0:T(8,128)(2,1)S(1)}, bf16[2,35,512]{2,1,0:T(8,128)(2,1)S(1)}, u32[]{:S(2)}, u32[]{:S(2)}) collective-permute-start(bf16[2,35,512]{2,1,0:T(8,128)(2,1)S(1)} %get-tuple-element.4), channel_id=1, source_target_pairs={{1,0},{2,1},{3,2},{5,4},{6,5},{7,6},{9,8},{10,9},{11,10},{13,12},{... | collective-permute-start | bytes 215048 | tf_op jit(solution)/shard_map/ppermute | solution.py:401
  52.1 3.1 %collective-permute-start.7 = (bf16[2,35,512]{2,1,0:T(8,128)(2,1)S(1)}, bf16[2,35,512]{2,1,0:T(8,128)(2,1)S(1)}, u32[]{:S(2)}, u32[]{:S(2)}) collective-permute-start(bf16[2,35,512]{2,1,0:T(8,128)(2,1)S(1)} %get-tuple-element.5), channel_id=1, source_target_pairs={{0,1},{1,2},{2,3},{4,5},{5,6},{6,7},{8,9},{9,10},{10,11},{12,13},{... | collective-permute-start | bytes 215048 | tf_op jit(solution)/shard_map/ppermute | solution.py:400
  55.3 0.7 pad_maximum_fusion.own
  56.0 0.0 collective-permute-done.8.high
  56.0 0.0 copy-start.1
  56.0 0.8 %collective-permute-done.7.low = bf16[2,35,512]{2,1,0:T(8,128)(2,1)S(1)} collective-permute-done((bf16[2,35,512]{2,1,0:T(8,128)(2,1)S(1)}, bf16[2,35,512]{2,1,0:T(8,128)(2,1)S(1)}, u32[]{:S(2)}, u32[]{:S(2)}) %collective-permute-start.7) | collective-permute-done | bytes 71712 | tf_op jit(solution)/shard_map/ppermute | solution.py:400
  56.7 0.0 copy-done.1
  56.7 0.0 copy-start.2
  56.7 0.6 copy-done.2
  57.4 14.8 %fine_step.1 = f32[2,35,8192]{2,1,0:T(8,128)} custom-call(s32[2]{0:T(128)} %add_convert_fusion.flags, f32[3]{0:T(128)} %velocity.3, bf16[2,35,1024]{2,1,0:T(8,128)(2,1)} %pad_maximum_fusion.own, bf16[2,35,512]{2,1,0:T(8,128)(2,1)} %copy-done.2, bf16[2,35,512]{2,1,0:T(8,128)(2,1)} %copy-done.1, bf16[256,2048]{1,0:T(8,128)(2,1)} %constant.103.clone.weights, ...), custom_call_target="tpu_custom_call" | custom-call | flops 4000000000 | bytes 8000000 | tf_op jit(solution)/shard_map/fine_step/pallas_call | solution.py:328
  72.2 4.9 %copy.14 = f32[2,35,8192]{2,0,1:T(2,128)} copy(f32[2,35,8192]{2,1,0:T(8,128)} %fine_step.1) | data formatting | bytes 4587520
  (4 shorter events, 0.1 us)
Async XLA Ops:
  0.6 49.0 %copy-start = (bf16[1,35,1024]{2,1,0:T(8,128)(2,1)S(1)}, bf16[1,35,1024]{2,1,0:T(8,128)(2,1)}, u32[]{:S(2)}) copy-start(bf16[1,35,1024]{2,1,0:T(8,128)(2,1)} %own.1) | copy-start | bytes 215044
  0.6 20.0 %collective-permute-start.6 = (bf16[1,35,1024]{2,1,0:T(8,128)(2,1)}, bf16[1,35,1024]{2,1,0:T(8,128)(2,1)S(1)}, u32[]{:S(2)}, u32[]{:S(2)}) collective-permute-start(bf16[1,35,1024]{2,1,0:T(8,128)(2,1)} %own.1), channel_id=1, source_target_pairs={{0,4},{4,8},{8,12},{12,16},{16,20},{20,24},{24,28},{28,0},{1,5},{5... | collective-permute-start | bytes 215048 | tf_op jit(solution)/shard_map/ppermute | solution.py:414
  2.8 19.0 %collective-permute-start.5 = (bf16[1,35,1024]{2,1,0:T(8,128)(2,1)}, bf16[1,35,1024]{2,1,0:T(8,128)(2,1)S(1)}, u32[]{:S(2)}, u32[]{:S(2)}) collective-permute-start(bf16[1,35,1024]{2,1,0:T(8,128)(2,1)} %own.1), channel_id=1, source_target_pairs={{0,8},{4,12},{8,16},{12,20},{16,24},{20,28},{24,0},{28,4},{1,9},{5... | collective-permute-start | bytes 215048 | tf_op jit(solution)/shard_map/ppermute | solution.py:414
  4.0 45.5 %collective-permute-start.4 = (bf16[1,35,1024]{2,1,0:T(8,128)(2,1)}, bf16[1,35,1024]{2,1,0:T(8,128)(2,1)S(1)}, u32[]{:S(2)}, u32[]{:S(2)}) collective-permute-start(bf16[1,35,1024]{2,1,0:T(8,128)(2,1)} %own.1), channel_id=1, source_target_pairs={{0,12},{4,16},{8,20},{12,24},{16,28},{20,0},{24,4},{28,8},{1,13},{... | collective-permute-start | bytes 215048 | tf_op jit(solution)/shard_map/ppermute | solution.py:414
  7.1 10.2 %collective-permute-start.10 = (bf16[1,35,512]{2,1,0:T(8,128)(2,1)S(1)}, bf16[1,35,512]{2,1,0:T(8,128)(2,1)S(1)}, u32[]{:S(2)}, u32[]{:S(2)}) collective-permute-start(bf16[1,35,512]{2,1,0:T(8,128)(2,1)S(1)} %get-tuple-element.6), channel_id=1, source_target_pairs={{1,0},{2,1},{3,2},{5,4},{6,5},{7,6},{9,8},{10,9},{11,10},{13,12},{... | collective-permute-start | bytes 107528 | tf_op jit(solution)/shard_map/ppermute | solution.py:401
  10.5 7.8 %collective-permute-start.9 = (bf16[1,35,512]{2,1,0:T(8,128)(2,1)S(1)}, bf16[1,35,512]{2,1,0:T(8,128)(2,1)S(1)}, u32[]{:S(2)}, u32[]{:S(2)}) collective-permute-start(bf16[1,35,512]{2,1,0:T(8,128)(2,1)S(1)} %get-tuple-element.7), channel_id=1, source_target_pairs={{0,1},{1,2},{2,3},{4,5},{5,6},{6,7},{8,9},{9,10},{10,11},{12,13},{... | collective-permute-start | bytes 107528 | tf_op jit(solution)/shard_map/ppermute | solution.py:400
  17.4 27.7 %copy-start.3 = (bf16[1,35,512]{2,1,0:T(8,128)(2,1)}, bf16[1,35,512]{2,1,0:T(8,128)(2,1)S(1)}, u32[]{:S(2)}) copy-start(bf16[1,35,512]{2,1,0:T(8,128)(2,1)S(1)} %collective-permute-done.10.high) | copy-start | bytes 107524
  17.4 32.2 %collective-permute-start.3 = (bf16[1,35,1024]{2,1,0:T(8,128)(2,1)}, bf16[1,35,1024]{2,1,0:T(8,128)(2,1)S(1)}, u32[]{:S(2)}, u32[]{:S(2)}) collective-permute-start(bf16[1,35,1024]{2,1,0:T(8,128)(2,1)} %own.1), channel_id=1, source_target_pairs={{0,16},{4,20},{8,24},{12,28},{16,0},{20,4},{24,8},{28,12},{1,17},{... | collective-permute-start | bytes 215048 | tf_op jit(solution)/shard_map/ppermute | solution.py:414
  18.3 26.7 %copy-start.4 = (bf16[1,35,512]{2,1,0:T(8,128)(2,1)}, bf16[1,35,512]{2,1,0:T(8,128)(2,1)S(1)}, u32[]{:S(2)}) copy-start(bf16[1,35,512]{2,1,0:T(8,128)(2,1)S(1)} %collective-permute-done.9.low) | copy-start | bytes 107524
  18.3 31.2 %collective-permute-start.2 = (bf16[1,35,1024]{2,1,0:T(8,128)(2,1)}, bf16[1,35,1024]{2,1,0:T(8,128)(2,1)S(1)}, u32[]{:S(2)}, u32[]{:S(2)}) collective-permute-start(bf16[1,35,1024]{2,1,0:T(8,128)(2,1)} %own.1), channel_id=1, source_target_pairs={{0,20},{4,24},{8,28},{12,0},{16,4},{20,8},{24,12},{28,16},{1,21},{... | collective-permute-start | bytes 215048 | tf_op jit(solution)/shard_map/ppermute | solution.py:414
  20.7 28.8 %collective-permute-start.1 = (bf16[1,35,1024]{2,1,0:T(8,128)(2,1)}, bf16[1,35,1024]{2,1,0:T(8,128)(2,1)S(1)}, u32[]{:S(2)}, u32[]{:S(2)}) collective-permute-start(bf16[1,35,1024]{2,1,0:T(8,128)(2,1)} %own.1), channel_id=1, source_target_pairs={{0,24},{4,28},{8,0},{12,4},{16,8},{20,12},{24,16},{28,20},{1,25},{... | collective-permute-start | bytes 215048 | tf_op jit(solution)/shard_map/ppermute | solution.py:414
  21.8 27.8 %collective-permute-start = (bf16[1,35,1024]{2,1,0:T(8,128)(2,1)}, bf16[1,35,1024]{2,1,0:T(8,128)(2,1)S(1)}, u32[]{:S(2)}, u32[]{:S(2)}) collective-permute-start(bf16[1,35,1024]{2,1,0:T(8,128)(2,1)} %own.1), channel_id=1, source_target_pairs={{0,28},{4,0},{8,4},{12,8},{16,12},{20,16},{24,20},{28,24},{1,29},{... | collective-permute-start | bytes 215048 | tf_op jit(solution)/shard_map/ppermute | solution.py:414
  49.7 6.3 %collective-permute-start.8 = (bf16[2,35,512]{2,1,0:T(8,128)(2,1)S(1)}, bf16[2,35,512]{2,1,0:T(8,128)(2,1)S(1)}, u32[]{:S(2)}, u32[]{:S(2)}) collective-permute-start(bf16[2,35,512]{2,1,0:T(8,128)(2,1)S(1)} %get-tuple-element.4), channel_id=1, source_target_pairs={{1,0},{2,1},{3,2},{5,4},{6,5},{7,6},{9,8},{10,9},{11,10},{13,12},{... | collective-permute-start | bytes 215048 | tf_op jit(solution)/shard_map/ppermute | solution.py:401
  52.1 4.6 %collective-permute-start.7 = (bf16[2,35,512]{2,1,0:T(8,128)(2,1)S(1)}, bf16[2,35,512]{2,1,0:T(8,128)(2,1)S(1)}, u32[]{:S(2)}, u32[]{:S(2)}) collective-permute-start(bf16[2,35,512]{2,1,0:T(8,128)(2,1)S(1)} %get-tuple-element.5), channel_id=1, source_target_pairs={{0,1},{1,2},{2,3},{4,5},{5,6},{6,7},{8,9},{9,10},{10,11},{12,13},{... | collective-permute-start | bytes 215048 | tf_op jit(solution)/shard_map/ppermute | solution.py:400
  56.0 0.8 %copy-start.1 = (bf16[2,35,512]{2,1,0:T(8,128)(2,1)}, bf16[2,35,512]{2,1,0:T(8,128)(2,1)S(1)}, u32[]{:S(2)}) copy-start(bf16[2,35,512]{2,1,0:T(8,128)(2,1)S(1)} %collective-permute-done.8.high) | copy-start | bytes 215044
  56.7 0.6 copy-start.2

commit v2 on v1

v2 whole, which is shorter than its diff:
```python
import functools

import jax
import jax.numpy as jnp
import numpy as np
from jax import lax
from jax.experimental import pallas as pl
from jax.experimental.pallas import tpu as pltpu
from jax.sharding import PartitionSpec as P

CB = 16
FINE = 2 * CB
CELLS = CB * CB
AREA = FINE * FINE
TILE = 128
DIRECT = 8

time_step = 0.25
heat_gain = 2.0


def interpolation():
    slope = np.zeros((CB, CB), np.float32)
    for i in range(1, CB - 1):
        slope[i + 1, i], slope[i - 1, i] = 0.5, -0.5
    slope[1, 0], slope[0, 0] = 1.0, -1.0
    slope[-1, -1], slope[-2, -1] = 1.0, -1.0
    copy = np.zeros((CB, FINE), np.float32)
    tilt = np.zeros((CB, FINE), np.float32)
    for i in range(CB):
        for a in range(2):
            copy[i, 2 * i + a] = 1.0
            tilt[:, 2 * i + a] = slope[:, i] * (a - 0.5) * 0.5
    same = np.kron(copy, copy)
    full = same + np.kron(copy, tilt) + np.kron(tilt, copy)
    return full, same


def strips():
    edge = np.arange(FINE)
    last = FINE - 1
    border = [edge * FINE, edge * FINE + last, edge, last * FINE + edge]
    inner = [edge * FINE + 1, edge * FINE + last - 1, FINE + edge, (last - 1) * FINE + edge]
    return np.concatenate(border), np.concatenate(inner)


def pair_sums(layers):
    place = np.zeros((layers * TILE, layers * TILE // 2), np.float32)
    for k in range(layers):
        for lane in range(TILE):
            place[k * TILE + lane, k * TILE // 2 + lane // 2] = 0.25
    return place


def up(value, unit):
    return -(-value // unit) * unit


def equal(shape, left, right):
    rows = lax.broadcasted_iota(jnp.int32, shape, 0)
    columns = lax.broadcasted_iota(jnp.int32, shape, 1)
    return left(rows) == right(columns)


def fill_coarse(stack, blocks, rows, layers):
    slots = len(blocks)
    fields = blocks[0].shape[0]
    mixed = None
    for s in range(slots):
        spot = equal((rows, fields), lambda r: r, lambda f: f * slots + s)
        part = jnp.dot(
            spot.astype(jnp.float32).astype(jnp.bfloat16),
            blocks[s],
            preferred_element_type=jnp.float32,
        )
        mixed = part if mixed is None else mixed + part
    pad = up(rows, 16)
    for k in range(layers + 4):
        stack[k * pad : k * pad + rows, :] = mixed[:, k * CELLS : (k + 1) * CELLS].astype(
            jnp.bfloat16
        )


def edge_ghosts(parts, bottom, top, layers, width, count):
    pad = up(count, 16)

    def rows(k):
        return slice((k + 2) * pad, (k + 2) * pad + count)

    @pl.when(bottom)
    def _():
        parts[rows(-1), width:] = 2.0 * parts[rows(0), width:] - parts[rows(1), width:]

    @pl.when(top)
    def _():
        parts[rows(layers), width:] = (
            2.0 * parts[rows(layers - 1), width:] - parts[rows(layers - 2), width:]
        )


def fine_layers(start, parts, layers, width, count):
    step = 2 * TILE
    pad = up(count, 16)

    def rows(k):
        return pl.ds(pl.multiple_of((k + 1) * pad, 16), count)

    def body(k, carry):
        for c in range(0, width, step):
            lanes = slice(c, c + step)
            copies = slice(width + c, width + c + step)
            centre = parts[rows(k), lanes]
            tilt = (parts[rows(k + 1), copies] - parts[rows(k - 1), copies]) * 0.125
            start[2 * k, :, lanes] = centre - tilt
            start[2 * k + 1, :, lanes] = centre + tilt
        return carry

    lax.fori_loop(0, layers + 2, body, 0)


def exact_dot(left, right):
    return jnp.dot(
        left, right, precision=lax.Precision.HIGHEST, preferred_element_type=jnp.float32
    )


def split_coupling(stoich, slots, rows):
    value = stoich[...]
    fields = value.shape[0]
    pad = up(rows, 16)
    width = 3 * pad
    rise = equal((rows, fields), lambda r: r // slots, lambda f: f).astype(jnp.float32)
    run = equal((fields, width), lambda f: f, lambda c: c % pad // slots).astype(jnp.float32)
    spread = exact_dot(rise, exact_dot(value, run))
    shape = (rows, width)
    spread = jnp.where(equal(shape, lambda r: r % slots, lambda c: c % pad % slots), spread, 0.0)
    head = spread.astype(jnp.bfloat16)
    rest = (spread - head.astype(jnp.float32)).astype(jnp.bfloat16)
    column = lax.broadcasted_iota(jnp.int32, shape, 1)
    return jnp.where(
        column < 2 * pad, head.astype(jnp.float32), rest.astype(jnp.float32)
    ).astype(jnp.bfloat16)


def spread_diffusivity(diffusivity, slots, rows):
    field = lax.broadcasted_iota(jnp.int32, (rows, TILE), 0) // slots
    value = jnp.zeros((rows, TILE), jnp.float32)
    for f in range(diffusivity.shape[0]):
        value = jnp.where(field == f, diffusivity[f], value)
    return value


def warmth(field, slots):
    warm = jax.nn.sigmoid(heat_gain * field[0:slots])
    row = lax.broadcasted_iota(jnp.int32, (8, field.shape[1]), 0) % slots
    value = jnp.broadcast_to(warm[0:1], row.shape)
    for s in range(1, slots):
        value = jnp.where(row == s, warm[s : s + 1], value)
    return value


def store_rate(rate, lanes, cells, warm):
    rows = cells.shape[0]
    pad = up(rows, 16)
    value = cells * jnp.concatenate([warm] * (rows // 8), 0)
    head = value.astype(jnp.bfloat16)
    rest = (value - head.astype(jnp.float32)).astype(jnp.bfloat16)
    rate[0:rows, lanes] = head
    rate[pad : pad + rows, lanes] = rest
    rate[2 * pad : 2 * pad + rows, lanes] = head


def sources(rate, mixed):
    return jnp.dot(mixed, rate[...], preferred_element_type=jnp.float32)


def stage(field, z, slots, rate, mixed, velocity, diffuse, emit):
    count = AREA // TILE
    lane = lax.broadcasted_iota(jnp.int32, diffuse.shape, 1)
    pos = lane % FINE
    at_low, at_high = pos == 0, pos == FINE - 1
    head, tail = lane < FINE, lane >= TILE - FINE
    half = [velocity[d] * 0.5 for d in range(3)]
    warm = warmth(field[z, 0:8, :], slots)
    for t in range(count):
        lanes = slice(t * TILE, (t + 1) * TILE)
        store_rate(rate, lanes, field[z, :, lanes], warm[:, lanes])
    source = sources(rate, mixed)
    tiles = {}
    ups = {}
    downs = {}

    def tile(t):
        if t not in tiles:
            tiles[t] = field[z, :, t * TILE : (t + 1) * TILE]
            ups[t] = pltpu.roll(tiles[t], TILE - FINE, 1)
            downs[t] = pltpu.roll(tiles[t], FINE, 1)
        return tiles[t]

    for t in range(count):
        lanes = slice(t * TILE, (t + 1) * TILE)
        cells = tile(t)
        x_low = jnp.where(at_low, cells, pltpu.roll(cells, 1, 1))
        x_high = jnp.where(at_high, cells, pltpu.roll(cells, TILE - 1, 1))
        if t + 1 < count:
            tile(t + 1)
        y_low = jnp.where(head, downs[t - 1] if t else cells, downs[t])
        y_high = jnp.where(tail, ups[t + 1] if t + 1 < count else cells, ups[t])
        z_low = field[z - 1, :, lanes]
        z_high = field[z + 1, :, lanes]
        drift = (
            half[0] * (x_high - x_low) + half[1] * (y_high - y_low) + half[2] * (z_high - z_low)
        )
        spread = (x_high + x_low) + (y_high + y_low) + (z_high + z_low) - 6.0 * cells
        emit(lanes, cells, source[:, lanes] - drift + diffuse * spread)


def step_kernel(layers, slots, direct, velocity, owner, stoich, diffusivity, weights, *refs):
    blocks = refs[:-7]
    out, picked, stack, parts, start, middle, rate = refs[-7:]
    pencil = lax.axis_index("gy")
    bottom, top = pencil == 0, pencil == lax.axis_size("gy") - 1
    depth = 2 * layers
    rows = start.shape[1]
    rate[...] = jnp.zeros_like(rate)
    if direct:
        groups = lax.axis_size("gx")
        group = lax.axis_index("gx")
        picked[...] = jnp.zeros_like(picked)
        for j, block in enumerate(blocks):
            origin = lax.rem(group - j + groups, groups)
            for t in range(block.shape[0]):
                slot = owner[origin * block.shape[0] + t] - group * slots
                for s in range(slots):

                    @pl.when(slot == s)
                    def _():
                        picked[s] = block[t]
    else:
        picked[...] = blocks[0][...]
    fill_coarse(stack, [picked[s] for s in range(slots)], rows, layers)
    parts[...] = jnp.dot(stack[...], weights[...], preferred_element_type=jnp.float32)
    edge_ghosts(parts, bottom, top, layers, AREA, rows)
    fine_layers(start, parts, layers, AREA, rows)

    @pl.when(bottom)
    def _():
        start[1] = start[2]

    @pl.when(top)
    def _():
        start[depth + 2] = start[depth + 1]

    mixed = split_coupling(stoich, slots, rows)
    diffuse = spread_diffusivity(diffusivity, slots, rows)

    def first(i, carry):
        def emit(lanes, cells, change):
            middle[i, :, lanes] = cells + time_step * change

        stage(start, i + 1, slots, rate, mixed, velocity, diffuse, emit)
        return carry

    lax.fori_loop(0, depth + 2, first, 0)

    @pl.when(bottom)
    def _():
        middle[0] = middle[1]

    @pl.when(top)
    def _():
        middle[depth + 1] = middle[depth]

    def second(i, carry):
        def emit(lanes, cells, change):
            value = (start[i + 2, :, lanes] + cells) * 0.5 + (time_step * 0.5) * change
            at = pl.multiple_of(i * AREA + lanes.start, TILE)
            for f in range(out.shape[0]):
                out[f, :, pl.ds(at, TILE)] = value[f * slots : (f + 1) * slots]

        stage(middle, i + 1, slots, rate, mixed, velocity, diffuse, emit)
        return carry

    lax.fori_loop(0, depth, second, 0)


def side_kernel(
    layers, velocity, stoich, diffusivity, weights, place, fluxes, block, out, stack, parts,
    start, rate, faces,
):
    pencil = lax.axis_index("gy")
    bottom, top = pencil == 0, pencil == lax.axis_size("gy") - 1
    fields = block.shape[1]
    depth = 2 * layers
    width = 2 * TILE
    rows = start.shape[1]
    rate[...] = jnp.zeros_like(rate)
    fill_coarse(stack, [block[0]], rows, layers)
    parts[...] = jnp.dot(stack[...], weights[...], preferred_element_type=jnp.float32)
    edge_ghosts(parts, bottom, top, layers, width, rows)
    fine_layers(start, parts, layers, width, rows)

    @pl.when(bottom)
    def _():
        start[1] = start[2]

    @pl.when(top)
    def _():
        start[depth + 2] = start[depth + 1]

    mixed = split_coupling(stoich, 1, rows)
    diffuse = spread_diffusivity(diffusivity, 1, rows)
    lane = lax.broadcasted_iota(jnp.int32, (rows, TILE), 1)
    pos = lane % FINE
    side = lane // FINE
    at_low, at_high = pos == 0, pos == FINE - 1
    normal = jnp.where(side < 2, velocity[0], velocity[1])
    along = jnp.where(side < 2, velocity[1], velocity[0]) * 0.5
    inward = jnp.where(side % 2 == 0, normal, -normal) * 0.5
    half_z = velocity[2] * 0.5
    border = slice(0, TILE)
    inner = slice(TILE, 2 * TILE)
    for i in range(depth):
        warm = warmth(start[i + 2, 0:8, border], 1)
        store_rate(rate, slice(i * TILE, (i + 1) * TILE), start[i + 2, :, border], warm)
    source = sources(rate, mixed)
    totals = []
    for i in range(depth):
        cells = start[i + 2, :, border]
        gap = start[i + 2, :, inner] - cells
        behind = jnp.where(at_low, cells, pltpu.roll(cells, 1, 1))
        ahead = jnp.where(at_high, cells, pltpu.roll(cells, TILE - 1, 1))
        z_low = start[i + 1, :, border]
        z_high = start[i + 3, :, border]
        drift = inward * gap + along * (ahead - behind) + half_z * (z_high - z_low)
        spread = gap + (ahead + behind) + (z_high + z_low) - 4.0 * cells
        change = source[:, i * TILE : (i + 1) * TILE] - drift + diffuse * spread
        later = cells + time_step * change
        totals.append((normal * cells + normal * later) * 0.5)
    for k in range(layers):
        faces[:, k * TILE : (k + 1) * TILE] = totals[2 * k] + totals[2 * k + 1]
    summed = exact_dot(faces[...], place[...])
    out[:, 0, :] = summed[:fields] - fluxes[:, 0, :]


def vmem(count):
    return [pl.BlockSpec(memory_space=pltpu.VMEM)] * count


def smem(count):
    return [pl.BlockSpec(memory_space=pltpu.SMEM)] * count


def fine_step(velocity, patch_owner, stoich, diffusivity, blocks, slots, direct):
    fields = blocks[0].shape[1]
    layers = blocks[0].shape[2] // CELLS - 4
    rows = up(slots * fields, 8)
    pad = up(rows, 16)
    full, same = interpolation()
    weights = jnp.asarray(np.concatenate([full, same], 1), jnp.bfloat16)
    cells = 2 * layers * AREA
    out = pl.pallas_call(
        functools.partial(step_kernel, layers, slots, direct),
        in_specs=smem(2) + vmem(1) + smem(1) + vmem(1 + len(blocks)),
        out_specs=pl.BlockSpec(memory_space=pltpu.VMEM),
        out_shape=jax.ShapeDtypeStruct((fields, slots, cells), jnp.float32),
        scratch_shapes=[
            pltpu.VMEM((slots,) + blocks[0].shape[1:], jnp.bfloat16),
            pltpu.VMEM(((layers + 4) * pad, CELLS), jnp.bfloat16),
            pltpu.VMEM(((layers + 4) * pad, 2 * AREA), jnp.float32),
            pltpu.VMEM((2 * layers + 4, rows, AREA), jnp.float32),
            pltpu.VMEM((2 * layers + 2, rows, AREA), jnp.float32),
            pltpu.VMEM((3 * pad, AREA), jnp.bfloat16),
        ],
        cost_estimate=pl.CostEstimate(
            flops=4000000000, bytes_accessed=8000000, transcendentals=0
        ),
        name="fine_step",
    )(velocity, patch_owner, stoich, diffusivity, weights, *blocks)
    return out.transpose(1, 0, 2)


def side_fluxes(velocity, stoich, diffusivity, block, fluxes):
    fields = block.shape[1]
    layers = block.shape[2] // CELLS - 4
    rows = up(fields, 8)
    pad = up(rows, 16)
    full, same = interpolation()
    border, inner = strips()
    picked = np.concatenate([border, inner])
    weights = jnp.asarray(np.concatenate([full[:, picked], same[:, picked]], 1), jnp.bfloat16)
    place = jnp.asarray(pair_sums(layers))
    return pl.pallas_call(
        functools.partial(side_kernel, layers),
        in_specs=smem(1) + vmem(1) + smem(1) + vmem(4),
        out_specs=pl.BlockSpec(memory_space=pltpu.VMEM),
        out_shape=jax.ShapeDtypeStruct((fields, 1, fluxes.shape[2]), jnp.float32),
        scratch_shapes=[
            pltpu.VMEM(((layers + 4) * pad, CELLS), jnp.bfloat16),
            pltpu.VMEM(((layers + 4) * pad, 4 * TILE), jnp.float32),
            pltpu.VMEM((2 * layers + 4, rows, 2 * TILE), jnp.float32),
            pltpu.VMEM((3 * pad, 2 * layers * TILE), jnp.bfloat16),
            pltpu.VMEM((rows, layers * TILE), jnp.float32),
        ],
        cost_estimate=pl.CostEstimate(
            flops=800000000, bytes_accessed=2000000, transcendentals=0
        ),
        name="side_fluxes",
    )(velocity, stoich, diffusivity, weights, place, fluxes.transpose(1, 0, 2), block).transpose(
        1, 0, 2
    )


def with_halo(block):
    count = lax.axis_size("gy")
    forward = [(i, i + 1) for i in range(count - 1)]
    backward = [(i + 1, i) for i in range(count - 1)]
    low = lax.ppermute(block[:, :, -2 * CELLS :], "gy", forward)
    high = lax.ppermute(block[:, :, : 2 * CELLS], "gy", backward)
    return jnp.concatenate([low, block, high], 2)


def fetch(block, patch_owner, slots):
    groups = lax.axis_size("gx")
    if groups > DIRECT:
        my_slots = lax.axis_index("gx") * slots + jnp.arange(slots, dtype=jnp.int32)
        chooser = (my_slots[:, None] == patch_owner[None, :]).astype(block.dtype)
        everything = lax.all_gather(block, "gx", axis=0, tiled=True)
        return [jnp.einsum("oq,qfc->ofc", chooser, everything)], False
    blocks = [block] + [
        lax.ppermute(block, "gx", [(i, (i + shift) % groups) for i in range(groups)])
        for shift in range(1, groups)
    ]
    return blocks, True


def shards(coarse_send, coarse_flux, patch_owner, velocity, diffusivity, stoich):
    send_slots = coarse_send.shape[0]
    slots = 2 * send_slots
    block = with_halo(coarse_send)
    blocks, direct = fetch(block, patch_owner, slots)
    reflux = [
        side_fluxes(velocity, stoich, diffusivity, block[s : s + 1], coarse_flux[s : s + 1])
        for s in range(send_slots)
    ]
    fine_state = fine_step(velocity, patch_owner, stoich, diffusivity, blocks, slots, direct)
    return fine_state, jnp.concatenate(reflux, 0)


def solution(mesh):
    placed = (P("gx", None, "gy"), P("gx", None, "gy"), P(), P(), P(), P())
    return jax.shard_map(
        shards,
        mesh=mesh,
        in_specs=placed,
        out_specs=(P("gx", None, "gy"), P("gx", None, "gy")),
        check_vma=False,
    )
```

time: 77.9 us -> 56.6 us (0.73)
  the two profiles are of different devices: /device:TPU:1 before, /device:TPU:13 now
where the time goes in v2:
time: 56.6 us; the launch traced here: 56.2 us
  waiting for transfers between devices  23.1 us (41%)
  Pallas kernels  17.3 us (31%)
  starting transfers between devices  12.7 us (22%)
  local copies, waits for them, and re-layouts  2.4 us (4%)
  between operations  0.71 us (1%)
    ppermute x7, waiting for transfers between devices, fetch(): lax.ppermute(block, 'gx', [(i, (i + shift) % groups) for i in range(group...  20.7 us
    pallas_call x1, Pallas kernels, fine_step(): pl.pallas_call(functools.partial(step_kernel, layers, slots, direct), in_...  13.9 us
    ppermute x7, starting transfers between devices, fetch(): lax.ppermute(block, 'gx', [(i, (i + shift) % groups) for i in range(group...  7.1 us
    ppermute x1, starting transfers between devices, with_halo(): low = lax.ppermute(block[:, :, -2 * CELLS:], 'gy', forward)  3.67 us
    pallas_call x1, Pallas kernels, side_fluxes(): pl.pallas_call(functools.partial(side_kernel, layers), in_specs=smem(1) +...  3.44 us
    ppermute x1, waiting for transfers between devices, with_halo(): high = lax.ppermute(block[:, :, :2 * CELLS], 'gy', backward)  2.47 us
    ppermute x1, starting transfers between devices, with_halo(): high = lax.ppermute(block[:, :, :2 * CELLS], 'gy', backward)  1.92 us
    unnamed x18, local copies, waits for them, and re-layouts  1.59 us
  transfers between devices with their start and end apart: 9, of which 6 were waited for; matrix products, arithmetic and copies ran while one was open for 2% of the time, Pallas kernels for 6%

profile of v2, /device:TPU:13, one launch (start us, length us, event | category | flops | bytes accessed | tf_op | source)
XLA Modules:
  0.0 56.2 jit_solution(7467489616039614350)
XLA Ops:
  0.6 0.8 %fusion = (bf16[1,35,512]{2,1,0:T(8,128)(2,1)S(1)}, bf16[1,35,512]{2,1,0:T(8,128)(2,1)S(1)}) fusion(bf16[1,35,1024]{2,1,0:T(8,128)(2,1)} %param.9), kind=kLoop, calls=%fused_computation.3 | loop fusion | bytes 143360 | tf_op jit(solution)/shard_map/slice | solution.py:419
  1.4 3.7 %collective-permute-start = (bf16[1,35,512]{2,1,0:T(8,128)(2,1)S(1)}, bf16[1,35,512]{2,1,0:T(8,128)(2,1)S(1)}, u32[]{:S(2)}, u32[]{:S(2)}) collective-permute-start(bf16[1,35,512]{2,1,0:T(8,128)(2,1)S(1)} %get-tuple-element.3), channel_id=1, source_target_pairs={{0,1},{1,2},{2,3},{4,5},{5,6},{6,7},{8,9},{9,10},{10,11},{12,13},{... | collective-permute-start | bytes 107528 | tf_op jit(solution)/shard_map/ppermute | solution.py:418
  5.1 1.9 %collective-permute-start.1 = (bf16[1,35,512]{2,1,0:T(8,128)(2,1)S(1)}, bf16[1,35,512]{2,1,0:T(8,128)(2,1)S(1)}, u32[]{:S(2)}, u32[]{:S(2)}) collective-permute-start(bf16[1,35,512]{2,1,0:T(8,128)(2,1)S(1)} %get-tuple-element.2), channel_id=1, source_target_pairs={{1,0},{2,1},{3,2},{5,4},{6,5},{7,6},{9,8},{10,9},{11,10},{13,12},{... | collective-permute-start | bytes 107528 | tf_op jit(solution)/shard_map/ppermute | solution.py:419
  7.0 0.0 collective-permute-done
  7.1 0.9 %constant_dynamic-update-slice_fusion.1 = bf16[1,35,2048]{2,1,0:T(8,128)(2,1)S(1)} fusion(bf16[1,35,2048]{2,1,0:T(8,128)(2,1)S(1)} %constant_dynamic-update-slice_fusion.2, bf16[1,35,1024]{2,1,0:T(8,128)(2,1)} %param.9), kind=kLoop, calls=%fused_computation.1 | loop fusion | bytes 153600
  8.0 2.5 %collective-permute-done.1 = bf16[1,35,512]{2,1,0:T(8,128)(2,1)S(1)} collective-permute-done((bf16[1,35,512]{2,1,0:T(8,128)(2,1)S(1)}, bf16[1,35,512]{2,1,0:T(8,128)(2,1)S(1)}, u32[]{:S(2)}, u32[]{:S(2)}) %collective-permute-start.1) | collective-permute-done | bytes 35872 | tf_op jit(solution)/shard_map/ppermute | solution.py:419
  10.4 0.0 copy-start
  10.4 1.2 %collective-permute-start.2 = (bf16[1,35,2048]{2,1,0:T(8,128)(2,1)S(1)}, bf16[1,35,2048]{2,1,0:T(8,128)(2,1)S(1)}, u32[]{:S(2)}, u32[]{:S(2)}) collective-permute-start(bf16[1,35,2048]{2,1,0:T(8,128)(2,1)S(1)} %constant_dynamic-update-slice_fusion.refs_0_.block), channel_id=1, source_target_pairs={{0,4},{4,8},{8,12},{12,16},{16,20},{20,24},{24,28},{28,0},{1,5},{5... | collective-permute-start | bytes 430088 | tf_op jit(solution)/shard_map/ppermute | solution.py:431
  11.7 1.3 %collective-permute-start.3 = (bf16[1,35,2048]{2,1,0:T(8,128)(2,1)S(1)}, bf16[1,35,2048]{2,1,0:T(8,128)(2,1)S(1)}, u32[]{:S(2)}, u32[]{:S(2)}) collective-permute-start(bf16[1,35,2048]{2,1,0:T(8,128)(2,1)S(1)} %constant_dynamic-update-slice_fusion.refs_0_.block), channel_id=1, source_target_pairs={{0,8},{4,12},{8,16},{12,20},{16,24},{20,28},{24,0},{28,4},{1,9},{5... | collective-permute-start | bytes 430088 | tf_op jit(solution)/shard_map/ppermute | solution.py:431
  13.0 1.0 %collective-permute-start.4 = (bf16[1,35,2048]{2,1,0:T(8,128)(2,1)S(1)}, bf16[1,35,2048]{2,1,0:T(8,128)(2,1)S(1)}, u32[]{:S(2)}, u32[]{:S(2)}) collective-permute-start(bf16[1,35,2048]{2,1,0:T(8,128)(2,1)S(1)} %constant_dynamic-update-slice_fusion.refs_0_.block), channel_id=1, source_target_pairs={{0,12},{4,16},{8,20},{12,24},{16,28},{20,0},{24,4},{28,8},{1,13},{... | collective-permute-start | bytes 430088 | tf_op jit(solution)/shard_map/ppermute | solution.py:431
  13.9 1.3 %collective-permute-start.5 = (bf16[1,35,2048]{2,1,0:T(8,128)(2,1)S(1)}, bf16[1,35,2048]{2,1,0:T(8,128)(2,1)S(1)}, u32[]{:S(2)}, u32[]{:S(2)}) collective-permute-start(bf16[1,35,2048]{2,1,0:T(8,128)(2,1)S(1)} %constant_dynamic-update-slice_fusion.refs_0_.block), channel_id=1, source_target_pairs={{0,16},{4,20},{8,24},{12,28},{16,0},{20,4},{24,8},{28,12},{1,17},{... | collective-permute-start | bytes 430088 | tf_op jit(solution)/shard_map/ppermute | solution.py:431
  15.3 1.0 %collective-permute-start.6 = (bf16[1,35,2048]{2,1,0:T(8,128)(2,1)S(1)}, bf16[1,35,2048]{2,1,0:T(8,128)(2,1)S(1)}, u32[]{:S(2)}, u32[]{:S(2)}) collective-permute-start(bf16[1,35,2048]{2,1,0:T(8,128)(2,1)S(1)} %constant_dynamic-update-slice_fusion.refs_0_.block), channel_id=1, source_target_pairs={{0,20},{4,24},{8,28},{12,0},{16,4},{20,8},{24,12},{28,16},{1,21},{... | collective-permute-start | bytes 430088 | tf_op jit(solution)/shard_map/ppermute | solution.py:431
  16.3 0.0 collective-permute-done.2.refs_1_
  16.3 0.0 copy-start.1
  16.3 1.2 %collective-permute-start.7 = (bf16[1,35,2048]{2,1,0:T(8,128)(2,1)S(1)}, bf16[1,35,2048]{2,1,0:T(8,128)(2,1)S(1)}, u32[]{:S(2)}, u32[]{:S(2)}) collective-permute-start(bf16[1,35,2048]{2,1,0:T(8,128)(2,1)S(1)} %constant_dynamic-update-slice_fusion.refs_0_.block), channel_id=1, source_target_pairs={{0,24},{4,28},{8,0},{12,4},{16,8},{20,12},{24,16},{28,20},{1,25},{... | collective-permute-start | bytes 430088 | tf_op jit(solution)/shard_map/ppermute | solution.py:431
  17.5 15.7 %collective-permute-done.3.refs_2_ = bf16[1,35,2048]{2,1,0:T(8,128)(2,1)S(1)} collective-permute-done((bf16[1,35,2048]{2,1,0:T(8,128)(2,1)S(1)}, bf16[1,35,2048]{2,1,0:T(8,128)(2,1)S(1)}, u32[]{:S(2)}, u32[]{:S(2)}) %collective-permute-start.3) | collective-permute-done | bytes 143392 | tf_op jit(solution)/shard_map/ppermute | solution.py:431
  33.3 0.0 copy-start.2
  33.3 0.0 collective-permute-start.8
  33.3 0.0 copy-done
  33.3 3.4 %side_fluxes.1 = f32[35,1,256]{2,1,0:T(1,128)} custom-call(f32[3]{0:T(128)} %velocity.3, f32[35,35]{1,0:T(8,128)} %stoich.3, f32[35]{0:T(128)} %diffusivity.3, bf16[256,512]{1,0:T(8,128)(2,1)} %constant.6.clone.weights, f32[512,256]{1,0:T(8,128)} %constant.7.clone.place, f32[35,1,256]{2,1,0:T(1,128)} %bitcast.3, bf16[1,35,2048]{2,1,0:T(8,128)(2,1)} %copy-done), custom_call_target="tpu_custom_call" | custom-call | flops 800000000 | bytes 2000000 | tf_op jit(solution)/shard_map/side_fluxes/pallas_call | solution.py:393
  36.7 0.1 collective-permute-done.4.refs_3_
  36.8 0.0 copy-start.3
  36.8 1.8 %collective-permute-done.5.refs_4_ = bf16[1,35,2048]{2,1,0:T(8,128)(2,1)S(1)} collective-permute-done((bf16[1,35,2048]{2,1,0:T(8,128)(2,1)S(1)}, bf16[1,35,2048]{2,1,0:T(8,128)(2,1)S(1)}, u32[]{:S(2)}, u32[]{:S(2)}) %collective-permute-start.5) | collective-permute-done | bytes 143392 | tf_op jit(solution)/shard_map/ppermute | solution.py:431
  38.5 0.0 copy-start.4
  38.5 0.0 collective-permute-done.6.refs_5_
  38.5 0.0 copy-start.5
  38.5 1.7 %collective-permute-done.7.refs_6_ = bf16[1,35,2048]{2,1,0:T(8,128)(2,1)S(1)} collective-permute-done((bf16[1,35,2048]{2,1,0:T(8,128)(2,1)S(1)}, bf16[1,35,2048]{2,1,0:T(8,128)(2,1)S(1)}, u32[]{:S(2)}, u32[]{:S(2)}) %collective-permute-start.7) | collective-permute-done | bytes 143392 | tf_op jit(solution)/shard_map/ppermute | solution.py:431
  40.3 0.0 copy-start.6
  40.3 1.4 %collective-permute-done.8.refs_7_ = bf16[1,35,2048]{2,1,0:T(8,128)(2,1)S(1)} collective-permute-done((bf16[1,35,2048]{2,1,0:T(8,128)(2,1)S(1)}, bf16[1,35,2048]{2,1,0:T(8,128)(2,1)S(1)}, u32[]{:S(2)}, u32[]{:S(2)}) %collective-permute-start.8) | collective-permute-done | bytes 143392 | tf_op jit(solution)/shard_map/ppermute | solution.py:431
  41.7 0.0 copy-done.1
  41.7 0.0 copy-done.2
  41.7 0.0 copy-done.3
  41.7 0.0 copy-done.4
  41.7 0.0 copy-done.5
  41.7 0.0 copy-done.6
  41.7 0.0 copy-start.7
  41.7 0.7 %copy-done.7 = bf16[1,35,2048]{2,1,0:T(8,128)(2,1)} copy-done((bf16[1,35,2048]{2,1,0:T(8,128)(2,1)}, bf16[1,35,2048]{2,1,0:T(8,128)(2,1)S(1)}, u32[]{:S(2)}) %copy-start.7) | copy-done | bytes 143384
  42.4 13.9 %fine_step.1 = f32[35,2,8192]{2,1,0:T(2,128)} custom-call(f32[3]{0:T(128)} %velocity.3, s32[8]{0:T(128)} %owner.1, f32[35,35]{1,0:T(8,128)} %stoich.3, f32[35]{0:T(128)} %diffusivity.3, bf16[256,2048]{1,0:T(8,128)(2,1)} %constant.8.clone.weights, bf16[1,35,2048]{2,1,0:T(8,128)(2,1)} %copy-done, bf16[1,35,2048]{2,1,0:T(8,128)(2,1)} %copy-done.1, ...), custom_call_target="tpu_custom_call" | custom-call | flops 4000000000 | bytes 8000000 | tf_op jit(solution)/shard_map/fine_step/pallas_call | solution.py:362
  (2 shorter events, 0.0 us)
Async XLA Ops:
  1.4 5.6 %collective-permute-start = (bf16[1,35,512]{2,1,0:T(8,128)(2,1)S(1)}, bf16[1,35,512]{2,1,0:T(8,128)(2,1)S(1)}, u32[]{:S(2)}, u32[]{:S(2)}) collective-permute-start(bf16[1,35,512]{2,1,0:T(8,128)(2,1)S(1)} %get-tuple-element.3), channel_id=1, source_target_pairs={{0,1},{1,2},{2,3},{4,5},{5,6},{6,7},{8,9},{9,10},{10,11},{12,13},{... | collective-permute-start | bytes 107528 | tf_op jit(solution)/shard_map/ppermute | solution.py:418
  5.1 5.3 %collective-permute-start.1 = (bf16[1,35,512]{2,1,0:T(8,128)(2,1)S(1)}, bf16[1,35,512]{2,1,0:T(8,128)(2,1)S(1)}, u32[]{:S(2)}, u32[]{:S(2)}) collective-permute-start(bf16[1,35,512]{2,1,0:T(8,128)(2,1)S(1)} %get-tuple-element.2), channel_id=1, source_target_pairs={{1,0},{2,1},{3,2},{5,4},{6,5},{7,6},{9,8},{10,9},{11,10},{13,12},{... | collective-permute-start | bytes 107528 | tf_op jit(solution)/shard_map/ppermute | solution.py:419
  10.4 22.8 %copy-start = (bf16[1,35,2048]{2,1,0:T(8,128)(2,1)}, bf16[1,35,2048]{2,1,0:T(8,128)(2,1)S(1)}, u32[]{:S(2)}) copy-start(bf16[1,35,2048]{2,1,0:T(8,128)(2,1)S(1)} %constant_dynamic-update-slice_fusion.refs_0_.block) | copy-start | bytes 430084
  10.4 5.9 %collective-permute-start.2 = (bf16[1,35,2048]{2,1,0:T(8,128)(2,1)S(1)}, bf16[1,35,2048]{2,1,0:T(8,128)(2,1)S(1)}, u32[]{:S(2)}, u32[]{:S(2)}) collective-permute-start(bf16[1,35,2048]{2,1,0:T(8,128)(2,1)S(1)} %constant_dynamic-update-slice_fusion.refs_0_.block), channel_id=1, source_target_pairs={{0,4},{4,8},{8,12},{12,16},{16,20},{20,24},{24,28},{28,0},{1,5},{5... | collective-permute-start | bytes 430088 | tf_op jit(solution)/shard_map/ppermute | solution.py:431
  11.7 21.6 %collective-permute-start.3 = (bf16[1,35,2048]{2,1,0:T(8,128)(2,1)S(1)}, bf16[1,35,2048]{2,1,0:T(8,128)(2,1)S(1)}, u32[]{:S(2)}, u32[]{:S(2)}) collective-permute-start(bf16[1,35,2048]{2,1,0:T(8,128)(2,1)S(1)} %constant_dynamic-update-slice_fusion.refs_0_.block), channel_id=1, source_target_pairs={{0,8},{4,12},{8,16},{12,20},{16,24},{20,28},{24,0},{28,4},{1,9},{5... | collective-permute-start | bytes 430088 | tf_op jit(solution)/shard_map/ppermute | solution.py:431
  13.0 23.8 %collective-permute-start.4 = (bf16[1,35,2048]{2,1,0:T(8,128)(2,1)S(1)}, bf16[1,35,2048]{2,1,0:T(8,128)(2,1)S(1)}, u32[]{:S(2)}, u32[]{:S(2)}) collective-permute-start(bf16[1,35,2048]{2,1,0:T(8,128)(2,1)S(1)} %constant_dynamic-update-slice_fusion.refs_0_.block), channel_id=1, source_target_pairs={{0,12},{4,16},{8,20},{12,24},{16,28},{20,0},{24,4},{28,8},{1,13},{... | collective-permute-start | bytes 430088 | tf_op jit(solution)/shard_map/ppermute | solution.py:431
  13.9 24.6 %collective-permute-start.5 = (bf16[1,35,2048]{2,1,0:T(8,128)(2,1)S(1)}, bf16[1,35,2048]{2,1,0:T(8,128)(2,1)S(1)}, u32[]{:S(2)}, u32[]{:S(2)}) collective-permute-start(bf16[1,35,2048]{2,1,0:T(8,128)(2,1)S(1)} %constant_dynamic-update-slice_fusion.refs_0_.block), channel_id=1, source_target_pairs={{0,16},{4,20},{8,24},{12,28},{16,0},{20,4},{24,8},{28,12},{1,17},{... | collective-permute-start | bytes 430088 | tf_op jit(solution)/shard_map/ppermute | solution.py:431
  15.3 23.3 %collective-permute-start.6 = (bf16[1,35,2048]{2,1,0:T(8,128)(2,1)S(1)}, bf16[1,35,2048]{2,1,0:T(8,128)(2,1)S(1)}, u32[]{:S(2)}, u32[]{:S(2)}) collective-permute-start(bf16[1,35,2048]{2,1,0:T(8,128)(2,1)S(1)} %constant_dynamic-update-slice_fusion.refs_0_.block), channel_id=1, source_target_pairs={{0,20},{4,24},{8,28},{12,0},{16,4},{20,8},{24,12},{28,16},{1,21},{... | collective-permute-start | bytes 430088 | tf_op jit(solution)/shard_map/ppermute | solution.py:431
  16.3 25.4 %copy-start.1 = (bf16[1,35,2048]{2,1,0:T(8,128)(2,1)}, bf16[1,35,2048]{2,1,0:T(8,128)(2,1)S(1)}, u32[]{:S(2)}) copy-start(bf16[1,35,2048]{2,1,0:T(8,128)(2,1)S(1)} %collective-permute-done.2.refs_1_) | copy-start | bytes 430084
  16.3 24.0 %collective-permute-start.7 = (bf16[1,35,2048]{2,1,0:T(8,128)(2,1)S(1)}, bf16[1,35,2048]{2,1,0:T(8,128)(2,1)S(1)}, u32[]{:S(2)}, u32[]{:S(2)}) collective-permute-start(bf16[1,35,2048]{2,1,0:T(8,128)(2,1)S(1)} %constant_dynamic-update-slice_fusion.refs_0_.block), channel_id=1, source_target_pairs={{0,24},{4,28},{8,0},{12,4},{16,8},{20,12},{24,16},{28,20},{1,25},{... | collective-permute-start | bytes 430088 | tf_op jit(solution)/shard_map/ppermute | solution.py:431
  33.3 8.4 %copy-start.2 = (bf16[1,35,2048]{2,1,0:T(8,128)(2,1)}, bf16[1,35,2048]{2,1,0:T(8,128)(2,1)S(1)}, u32[]{:S(2)}) copy-start(bf16[1,35,2048]{2,1,0:T(8,128)(2,1)S(1)} %collective-permute-done.3.refs_2_) | copy-start | bytes 430084
  33.3 8.4 %collective-permute-start.8 = (bf16[1,35,2048]{2,1,0:T(8,128)(2,1)S(1)}, bf16[1,35,2048]{2,1,0:T(8,128)(2,1)S(1)}, u32[]{:S(2)}, u32[]{:S(2)}) collective-permute-start(bf16[1,35,2048]{2,1,0:T(8,128)(2,1)S(1)} %constant_dynamic-update-slice_fusion.refs_0_.block), channel_id=1, source_target_pairs={{0,28},{4,0},{8,4},{12,8},{16,12},{20,16},{24,20},{28,24},{1,29},{... | collective-permute-start | bytes 430088 | tf_op jit(solution)/shard_map/ppermute | solution.py:431
  36.8 4.9 %copy-start.3 = (bf16[1,35,2048]{2,1,0:T(8,128)(2,1)}, bf16[1,35,2048]{2,1,0:T(8,128)(2,1)S(1)}, u32[]{:S(2)}) copy-start(bf16[1,35,2048]{2,1,0:T(8,128)(2,1)S(1)} %collective-permute-done.4.refs_3_) | copy-start | bytes 430084
  38.5 3.1 %copy-start.4 = (bf16[1,35,2048]{2,1,0:T(8,128)(2,1)}, bf16[1,35,2048]{2,1,0:T(8,128)(2,1)S(1)}, u32[]{:S(2)}) copy-start(bf16[1,35,2048]{2,1,0:T(8,128)(2,1)S(1)} %collective-permute-done.5.refs_4_) | copy-start | bytes 430084
  38.5 3.1 %copy-start.5 = (bf16[1,35,2048]{2,1,0:T(8,128)(2,1)}, bf16[1,35,2048]{2,1,0:T(8,128)(2,1)S(1)}, u32[]{:S(2)}) copy-start(bf16[1,35,2048]{2,1,0:T(8,128)(2,1)S(1)} %collective-permute-done.6.refs_5_) | copy-start | bytes 430084
  40.3 1.4 %copy-start.6 = (bf16[1,35,2048]{2,1,0:T(8,128)(2,1)}, bf16[1,35,2048]{2,1,0:T(8,128)(2,1)S(1)}, u32[]{:S(2)}) copy-start(bf16[1,35,2048]{2,1,0:T(8,128)(2,1)S(1)} %collective-permute-done.7.refs_6_) | copy-start | bytes 430084
  41.7 0.7 %copy-start.7 = (bf16[1,35,2048]{2,1,0:T(8,128)(2,1)}, bf16[1,35,2048]{2,1,0:T(8,128)(2,1)S(1)}, u32[]{:S(2)}) copy-start(bf16[1,35,2048]{2,1,0:T(8,128)(2,1)S(1)} %collective-permute-done.8.refs_7_) | copy-start | bytes 430084

commit v3 on v2

--- a/solution.py
+++ b/solution.py
@@ -215,29 +215,50 @@
         emit(lanes, cells, source[:, lanes] - drift + diffuse * spread)
 
 
-def step_kernel(layers, slots, direct, velocity, owner, stoich, diffusivity, weights, *refs):
-    blocks = refs[:-7]
+def join(picked, low, centres, high):
+    edge = 2 * CELLS
+    cells = centres[0].shape[2]
+    for s in range(picked.shape[0]):
+        picked[s, :, :edge] = low[s]
+        middle = centres[0][s]
+        for other in centres[1:]:
+            middle = middle + other[s]
+        picked[s, :, edge : edge + cells] = middle
+        picked[s, :, edge + cells :] = high[s]
+
+
+def pick_kernel(slots, owner, *refs):
+    blocks = refs[:-2]
+    mine, theirs = refs[-2:]
+    groups = lax.axis_size("gx")
+    group = lax.axis_index("gx")
+    partner = group + 1 - 2 * lax.rem(group, 2)
+    mine[...] = jnp.zeros_like(mine)
+    theirs[...] = jnp.zeros_like(theirs)
+    for j, block in enumerate(blocks):
+        origin = lax.rem(group - 2 * j + groups, groups)
+        for t in range(block.shape[0]):
+            slot = owner[origin * block.shape[0] + t]
+            for s in range(slots):
+
+                @pl.when(slot == group * slots + s)
+                def _():
+                    mine[s] = block[t]
+
+                @pl.when(slot == partner * slots + s)
+                def _():
+                    theirs[s] = block[t]
+
+
+def step_kernel(layers, slots, velocity, stoich, diffusivity, weights, *refs):
+    low, high, *centres = refs[:-7]
     out, picked, stack, parts, start, middle, rate = refs[-7:]
     pencil = lax.axis_index("gy")
     bottom, top = pencil == 0, pencil == lax.axis_size("gy") - 1
     depth = 2 * layers
     rows = start.shape[1]
     rate[...] = jnp.zeros_like(rate)
-    if direct:
-        groups = lax.axis_size("gx")
-        group = lax.axis_index("gx")
-        picked[...] = jnp.zeros_like(picked)
-        for j, block in enumerate(blocks):
-            origin = lax.rem(group - j + groups, groups)
-            for t in range(block.shape[0]):
-                slot = owner[origin * block.shape[0] + t] - group * slots
-                for s in range(slots):
-
-                    @pl.when(slot == s)
-                    def _():
-                        picked[s] = block[t]
-    else:
-        picked[...] = blocks[0][...]
+    join(picked, low, centres, high)
     fill_coarse(stack, [picked[s] for s in range(slots)], rows, layers)
     parts[...] = jnp.dot(stack[...], weights[...], preferred_element_type=jnp.float32)
     edge_ghosts(parts, bottom, top, layers, AREA, rows)
@@ -285,17 +306,18 @@
 
 
 def side_kernel(
-    layers, velocity, stoich, diffusivity, weights, place, fluxes, block, out, stack, parts,
-    start, rate, faces,
+    layers, velocity, stoich, diffusivity, weights, place, fluxes, low, high, own, out, picked,
+    stack, parts, start, rate, faces,
 ):
     pencil = lax.axis_index("gy")
     bottom, top = pencil == 0, pencil == lax.axis_size("gy") - 1
-    fields = block.shape[1]
+    fields = own.shape[1]
     depth = 2 * layers
     width = 2 * TILE
     rows = start.shape[1]
     rate[...] = jnp.zeros_like(rate)
-    fill_coarse(stack, [block[0]], rows, layers)
+    join(picked, low, [own], high)
+    fill_coarse(stack, [picked[0]], rows, layers)
     parts[...] = jnp.dot(stack[...], weights[...], preferred_element_type=jnp.float32)
     edge_ghosts(parts, bottom, top, layers, width, rows)
     fine_layers(start, parts, layers, width, rows)
@@ -351,21 +373,21 @@
     return [pl.BlockSpec(memory_space=pltpu.SMEM)] * count
 
 
-def fine_step(velocity, patch_owner, stoich, diffusivity, blocks, slots, direct):
-    fields = blocks[0].shape[1]
-    layers = blocks[0].shape[2] // CELLS - 4
+def fine_step(velocity, stoich, diffusivity, low, high, centres):
+    slots, fields, cells = centres[0].shape
+    layers = cells // CELLS
     rows = up(slots * fields, 8)
     pad = up(rows, 16)
     full, same = interpolation()
     weights = jnp.asarray(np.concatenate([full, same], 1), jnp.bfloat16)
     cells = 2 * layers * AREA
     out = pl.pallas_call(
-        functools.partial(step_kernel, layers, slots, direct),
-        in_specs=smem(2) + vmem(1) + smem(1) + vmem(1 + len(blocks)),
+        functools.partial(step_kernel, layers, slots),
+        in_specs=smem(1) + vmem(1) + smem(1) + vmem(3 + len(centres)),
         out_specs=pl.BlockSpec(memory_space=pltpu.VMEM),
         out_shape=jax.ShapeDtypeStruct((fields, slots, cells), jnp.float32),
         scratch_shapes=[
-            pltpu.VMEM((slots,) + blocks[0].shape[1:], jnp.bfloat16),
+            pltpu.VMEM((slots, fields, (layers + 4) * CELLS), jnp.bfloat16),
             pltpu.VMEM(((layers + 4) * pad, CELLS), jnp.bfloat16),
             pltpu.VMEM(((layers + 4) * pad, 2 * AREA), jnp.float32),
             pltpu.VMEM((2 * layers + 4, rows, AREA), jnp.float32),
@@ -376,13 +398,13 @@
             flops=4000000000, bytes_accessed=8000000, transcendentals=0
         ),
         name="fine_step",
-    )(velocity, patch_owner, stoich, diffusivity, weights, *blocks)
+    )(velocity, stoich, diffusivity, weights, low, high, *centres)
     return out.transpose(1, 0, 2)
 
 
-def side_fluxes(velocity, stoich, diffusivity, block, fluxes):
-    fields = block.shape[1]
-    layers = block.shape[2] // CELLS - 4
+def side_fluxes(velocity, stoich, diffusivity, low, high, own, fluxes):
+    fields = own.shape[1]
+    layers = own.shape[2] // CELLS
     rows = up(fields, 8)
     pad = up(rows, 16)
     full, same = interpolation()
@@ -392,10 +414,11 @@
     place = jnp.asarray(pair_sums(layers))
     return pl.pallas_call(
         functools.partial(side_kernel, layers),
-        in_specs=smem(1) + vmem(1) + smem(1) + vmem(4),
+        in_specs=smem(1) + vmem(1) + smem(1) + vmem(6),
         out_specs=pl.BlockSpec(memory_space=pltpu.VMEM),
         out_shape=jax.ShapeDtypeStruct((fields, 1, fluxes.shape[2]), jnp.float32),
         scratch_shapes=[
+            pltpu.VMEM((1, fields, (layers + 4) * CELLS), jnp.bfloat16),
             pltpu.VMEM(((layers + 4) * pad, CELLS), jnp.bfloat16),
             pltpu.VMEM(((layers + 4) * pad, 4 * TILE), jnp.float32),
             pltpu.VMEM((2 * layers + 4, rows, 2 * TILE), jnp.float32),
@@ -406,44 +429,56 @@
             flops=800000000, bytes_accessed=2000000, transcendentals=0
         ),
         name="side_fluxes",
-    )(velocity, stoich, diffusivity, weights, place, fluxes.transpose(1, 0, 2), block).transpose(
-        1, 0, 2
-    )
-
-
-def with_halo(block):
+    )(
+        velocity, stoich, diffusivity, weights, place, fluxes.transpose(1, 0, 2), low, high, own
+    ).transpose(1, 0, 2)
+
+
+def halo(blocks):
     count = lax.axis_size("gy")
     forward = [(i, i + 1) for i in range(count - 1)]
     backward = [(i + 1, i) for i in range(count - 1)]
-    low = lax.ppermute(block[:, :, -2 * CELLS :], "gy", forward)
-    high = lax.ppermute(block[:, :, : 2 * CELLS], "gy", backward)
-    return jnp.concatenate([low, block, high], 2)
-
-
-def fetch(block, patch_owner, slots):
+    last = sum(block[:, :, -2 * CELLS :] for block in blocks)
+    first = sum(block[:, :, : 2 * CELLS] for block in blocks)
+    return lax.ppermute(last, "gy", forward), lax.ppermute(first, "gy", backward)
+
+
+def fetch(own, patch_owner, slots):
     groups = lax.axis_size("gx")
-    if groups > DIRECT:
+    if groups > DIRECT or groups % 2:
         my_slots = lax.axis_index("gx") * slots + jnp.arange(slots, dtype=jnp.int32)
-        chooser = (my_slots[:, None] == patch_owner[None, :]).astype(block.dtype)
-        everything = lax.all_gather(block, "gx", axis=0, tiled=True)
-        return [jnp.einsum("oq,qfc->ofc", chooser, everything)], False
-    blocks = [block] + [
-        lax.ppermute(block, "gx", [(i, (i + shift) % groups) for i in range(groups)])
-        for shift in range(1, groups)
+        chooser = (my_slots[:, None] == patch_owner[None, :]).astype(own.dtype)
+        everything = lax.all_gather(own, "gx", axis=0, tiled=True)
+        return [jnp.einsum("oq,qfc->ofc", chooser, everything)]
+    blocks = [own] + [
+        lax.ppermute(own, "gx", [(i, (i + shift) % groups) for i in range(groups)])
+        for shift in range(2, groups, 2)
     ]
-    return blocks, True
+    shape = jax.ShapeDtypeStruct((slots,) + own.shape[1:], own.dtype)
+    mine, theirs = pl.pallas_call(
+        functools.partial(pick_kernel, slots),
+        in_specs=smem(1) + vmem(len(blocks)),
+        out_specs=vmem(2),
+        out_shape=[shape, shape],
+        cost_estimate=pl.CostEstimate(
+            flops=200000000, bytes_accessed=1000000, transcendentals=0
+        ),
+        name="pick",
+    )(patch_owner, *blocks)
+    return [mine, lax.ppermute(theirs, "gx", [(i, i ^ 1) for i in range(groups)])]
 
 
 def shards(coarse_send, coarse_flux, patch_owner, velocity, diffusivity, stoich):
     send_slots = coarse_send.shape[0]
-    slots = 2 * send_slots
-    block = with_halo(coarse_send)
-    blocks, direct = fetch(block, patch_owner, slots)
+    centres = fetch(coarse_send, patch_owner, 2 * send_slots)
+    low, high = halo([coarse_send])
     reflux = [
-        side_fluxes(velocity, stoich, diffusivity, block[s : s + 1], coarse_flux[s : s + 1])
+        side_fluxes(
+            velocity, stoich, diffusivity, *(a[s : s + 1] for a in (low, high, coarse_send, coarse_flux))
+        )
         for s in range(send_slots)
     ]
-    fine_state = fine_step(velocity, patch_owner, stoich, diffusivity, blocks, slots, direct)
+    fine_state = fine_step(velocity, stoich, diffusivity, *halo(centres), centres)
     return fine_state, jnp.concatenate(reflux, 0)
 
 

time: 56.6 us -> 48.3 us (0.85)
  the two profiles are of different devices: /device:TPU:13 before, /device:TPU:1 now
where the time goes in v3:
time: 48.3 us; the launch traced here: 47.9 us
  Pallas kernels  18.8 us (39%)
  starting transfers between devices  18.2 us (38%)
  waiting for transfers between devices  5.29 us (11%)
  local copies, waits for them, and re-layouts  3.9 us (8%)
  other arithmetic  1.01 us (2%)
  between operations  0.74 us (2%)
    pallas_call x1, Pallas kernels, fine_step(): pl.pallas_call(functools.partial(step_kernel, layers, slots), in_specs=sm...  13.5 us
    ppermute x2, starting transfers between devices, halo(): lax.ppermute(last, 'gy', forward)  7.69 us
    ppermute x3, starting transfers between devices, fetch(): lax.ppermute(own, 'gx', [(i, (i + shift) % groups) for i in range(groups)])  5.54 us
    ppermute x3, waiting for transfers between devices, fetch(): lax.ppermute(own, 'gx', [(i, (i + shift) % groups) for i in range(groups)])  5.28 us
    ppermute x2, starting transfers between devices, halo(): lax.ppermute(first, 'gy', backward)  3.84 us
    pallas_call x1, Pallas kernels, side_fluxes(): pl.pallas_call(functools.partial(side_kernel, layers), in_specs=smem(1) +...  3.42 us
    unnamed x16, local copies, waits for them, and re-layouts  3.09 us
    pallas_call x1, Pallas kernels, fetch(): pl.pallas_call(functools.partial(pick_kernel, slots), in_specs=smem(1) +...  1.85 us
  transfers between devices with their start and end apart: 8, of which 2 were waited for; matrix products, arithmetic and copies ran while one was open for 4% of the time, Pallas kernels for 7%

profile of v3, /device:TPU:1, one launch (start us, length us, event | category | flops | bytes accessed | tf_op | source)
XLA Modules:
  0.0 47.9 jit_solution(11530110071653412580)
XLA Ops:
  0.6 2.2 %collective-permute-start = (bf16[1,35,1024]{2,1,0:T(8,128)(2,1)}, bf16[1,35,1024]{2,1,0:T(8,128)(2,1)S(1)}, u32[]{:S(2)}, u32[]{:S(2)}) collective-permute-start(bf16[1,35,1024]{2,1,0:T(8,128)(2,1)} %own.1), channel_id=1, source_target_pairs={{0,8},{4,12},{8,16},{12,20},{16,24},{20,28},{24,0},{28,4},{1,9},{5... | collective-permute-start | bytes 215048 | tf_op jit(solution)/shard_map/ppermute | solution.py:454
  2.8 2.3 %collective-permute-start.1 = (bf16[1,35,1024]{2,1,0:T(8,128)(2,1)}, bf16[1,35,1024]{2,1,0:T(8,128)(2,1)S(1)}, u32[]{:S(2)}, u32[]{:S(2)}) collective-permute-start(bf16[1,35,1024]{2,1,0:T(8,128)(2,1)} %own.1), channel_id=1, source_target_pairs={{0,16},{4,20},{8,24},{12,28},{16,0},{20,4},{24,8},{28,12},{1,17},{... | collective-permute-start | bytes 215048 | tf_op jit(solution)/shard_map/ppermute | solution.py:454
  5.1 1.1 %collective-permute-start.2 = (bf16[1,35,1024]{2,1,0:T(8,128)(2,1)}, bf16[1,35,1024]{2,1,0:T(8,128)(2,1)S(1)}, u32[]{:S(2)}, u32[]{:S(2)}) collective-permute-start(bf16[1,35,1024]{2,1,0:T(8,128)(2,1)} %own.1), channel_id=1, source_target_pairs={{0,24},{4,28},{8,0},{12,4},{16,8},{20,12},{24,16},{28,20},{1,25},{... | collective-permute-start | bytes 215048 | tf_op jit(solution)/shard_map/ppermute | solution.py:454
  6.2 1.0 %collective-permute-done.refs_1_ = bf16[1,35,1024]{2,1,0:T(8,128)(2,1)S(1)} collective-permute-done((bf16[1,35,1024]{2,1,0:T(8,128)(2,1)}, bf16[1,35,1024]{2,1,0:T(8,128)(2,1)S(1)}, u32[]{:S(2)}, u32[]{:S(2)}) %collective-permute-start) | collective-permute-done | bytes 71712 | tf_op jit(solution)/shard_map/ppermute | solution.py:454
  7.2 0.0 copy-start.3
  7.2 4.3 %collective-permute-done.1.refs_2_ = bf16[1,35,1024]{2,1,0:T(8,128)(2,1)S(1)} collective-permute-done((bf16[1,35,1024]{2,1,0:T(8,128)(2,1)}, bf16[1,35,1024]{2,1,0:T(8,128)(2,1)S(1)}, u32[]{:S(2)}, u32[]{:S(2)}) %collective-permute-start.1) | collective-permute-done | bytes 71712 | tf_op jit(solution)/shard_map/ppermute | solution.py:454
  11.5 0.0 copy-start.4
  11.5 0.0 collective-permute-done.2.refs_3_
  11.5 0.0 copy-done.3
  11.5 0.6 %copy-done.4 = bf16[1,35,1024]{2,1,0:T(8,128)(2,1)} copy-done((bf16[1,35,1024]{2,1,0:T(8,128)(2,1)}, bf16[1,35,1024]{2,1,0:T(8,128)(2,1)S(1)}, u32[]{:S(2)}) %copy-start.4) | copy-done | bytes 71704
  12.1 0.0 copy-start.5
  12.1 0.6 %copy-done.5 = bf16[1,35,1024]{2,1,0:T(8,128)(2,1)} copy-done((bf16[1,35,1024]{2,1,0:T(8,128)(2,1)}, bf16[1,35,1024]{2,1,0:T(8,128)(2,1)S(1)}, u32[]{:S(2)}) %copy-start.5) | copy-done | bytes 71704
  12.7 1.9 %pick.1 = (bf16[2,35,1024]{2,1,0:T(8,128)(2,1)}, bf16[2,35,1024]{2,1,0:T(8,128)(2,1)}) custom-call(s32[8]{0:T(128)} %owner.1, bf16[1,35,1024]{2,1,0:T(8,128)(2,1)} %own.1, bf16[1,35,1024]{2,1,0:T(8,128)(2,1)} %copy-done.3, bf16[1,35,1024]{2,1,0:T(8,128)(2,1)} %copy-done.4, bf16[1,35,1024]{2,1,0:T(8,128)(2,1)} %copy-done.5), custom_call_target="tpu_custom_call" | custom-call | flops 200000000 | bytes 1000000 | tf_op jit(solution)/shard_map/pick/pallas_call | solution.py:458
  14.6 1.1 %collective-permute-start.3 = (bf16[2,35,1024]{2,1,0:T(8,128)(2,1)}, bf16[2,35,1024]{2,1,0:T(8,128)(2,1)S(1)}, u32[]{:S(2)}, u32[]{:S(2)}) collective-permute-start(bf16[2,35,1024]{2,1,0:T(8,128)(2,1)} %get-tuple-element.5), channel_id=1, source_target_pairs={{0,4},{4,0},{8,12},{12,8},{16,20},{20,16},{24,28},{28,24},{1,5},{5... | collective-permute-start | bytes 430088 | tf_op jit(solution)/shard_map/ppermute | solution.py:468
  15.7 0.8 %fusion = (bf16[1,35,512]{2,1,0:T(8,128)(2,1)S(1)}, bf16[1,35,512]{2,1,0:T(8,128)(2,1)S(1)}) fusion(bf16[1,35,1024]{2,1,0:T(8,128)(2,1)} %own.1), kind=kLoop, calls=%fused_computation.2 | loop fusion | bytes 143360 | tf_op jit(solution)/shard_map/slice | solution.py:442
  16.5 4.0 %collective-permute-start.6 = (bf16[1,35,512]{2,1,0:T(8,128)(2,1)S(1)}, bf16[1,35,512]{2,1,0:T(8,128)(2,1)S(1)}, u32[]{:S(2)}, u32[]{:S(2)}) collective-permute-start(bf16[1,35,512]{2,1,0:T(8,128)(2,1)S(1)} %get-tuple-element.9), channel_id=1, source_target_pairs={{0,1},{1,2},{2,3},{4,5},{5,6},{6,7},{8,9},{9,10},{10,11},{12,13},{... | collective-permute-start | bytes 107528 | tf_op jit(solution)/shard_map/ppermute | solution.py:443
  20.6 1.9 %collective-permute-start.7 = (bf16[1,35,512]{2,1,0:T(8,128)(2,1)S(1)}, bf16[1,35,512]{2,1,0:T(8,128)(2,1)S(1)}, u32[]{:S(2)}, u32[]{:S(2)}) collective-permute-start(bf16[1,35,512]{2,1,0:T(8,128)(2,1)S(1)} %get-tuple-element.8), channel_id=1, source_target_pairs={{1,0},{2,1},{3,2},{5,4},{6,5},{7,6},{9,8},{10,9},{11,10},{13,12},{... | collective-permute-start | bytes 107528 | tf_op jit(solution)/shard_map/ppermute | solution.py:443
  22.5 0.0 collective-permute-done.3.refs_3_
  22.5 0.0 copy-start
  22.5 1.0 %slice_add_fusion = (bf16[2,35,512]{2,1,0:T(8,128)(2,1)S(1)}, bf16[2,35,512]{2,1,0:T(8,128)(2,1)S(1)}) fusion(bf16[2,35,1024]{2,1,0:T(8,128)(2,1)S(1)} %collective-permute-done.3.refs_3_, bf16[2,35,1024]{2,1,0:T(8,128)(2,1)} %get-tuple-element.4.refs_2_), kind=kLoop, calls=%fused_computation | loop fusion | flops 71680 | bytes 430080 | tf_op jit(solution)/shard_map/add | solution.py:442
  23.5 3.6 %collective-permute-start.4 = (bf16[2,35,512]{2,1,0:T(8,128)(2,1)S(1)}, bf16[2,35,512]{2,1,0:T(8,128)(2,1)S(1)}, u32[]{:S(2)}, u32[]{:S(2)}) collective-permute-start(bf16[2,35,512]{2,1,0:T(8,128)(2,1)S(1)} %get-tuple-element.7), channel_id=1, source_target_pairs={{0,1},{1,2},{2,3},{4,5},{5,6},{6,7},{8,9},{9,10},{10,11},{12,13},{... | collective-permute-start | bytes 215048 | tf_op jit(solution)/shard_map/ppermute | solution.py:443
  27.2 1.9 %collective-permute-start.5 = (bf16[2,35,512]{2,1,0:T(8,128)(2,1)S(1)}, bf16[2,35,512]{2,1,0:T(8,128)(2,1)S(1)}, u32[]{:S(2)}, u32[]{:S(2)}) collective-permute-start(bf16[2,35,512]{2,1,0:T(8,128)(2,1)S(1)} %get-tuple-element.6), channel_id=1, source_target_pairs={{1,0},{2,1},{3,2},{5,4},{6,5},{7,6},{9,8},{10,9},{11,10},{13,12},{... | collective-permute-start | bytes 215048 | tf_op jit(solution)/shard_map/ppermute | solution.py:443
  29.1 0.0 collective-permute-done.6.low
  29.1 0.0 copy-start.6
  29.1 0.0 collective-permute-done.7.high
  29.1 0.0 copy-start.7
  29.2 0.6 %copy-done.6 = bf16[1,35,512]{2,1,0:T(8,128)(2,1)} copy-done((bf16[1,35,512]{2,1,0:T(8,128)(2,1)}, bf16[1,35,512]{2,1,0:T(8,128)(2,1)S(1)}, u32[]{:S(2)}) %copy-start.6) | copy-done | bytes 35864
  29.7 0.0 copy-done.7
  29.8 3.4 %side_fluxes.1 = f32[35,1,256]{2,1,0:T(1,128)} custom-call(f32[3]{0:T(128)} %velocity.3, f32[35,35]{1,0:T(8,128)} %stoich.3, f32[35]{0:T(128)} %diffusivity.3, bf16[256,512]{1,0:T(8,128)(2,1)} %constant.6.clone.weights, f32[512,256]{1,0:T(8,128)} %constant.7.clone.place, f32[35,1,256]{2,1,0:T(1,128)} %bitcast.3, bf16[1,35,512]{2,1,0:T(8,128)(2,1)} %copy-done.6, ...), custom_call_target="tpu_custom_call" | custom-call | flops 800000000 | bytes 2000000 | tf_op jit(solution)/shard_map/side_fluxes/pallas_call | solution.py:415
  33.2 0.0 collective-permute-done.4.refs_0_
  33.2 0.0 copy-start.1
  33.2 0.0 collective-permute-done.5.refs_1_
  33.2 0.0 copy-done
  33.2 0.6 %copy-done.1 = bf16[2,35,512]{2,1,0:T(8,128)(2,1)} copy-done((bf16[2,35,512]{2,1,0:T(8,128)(2,1)}, bf16[2,35,512]{2,1,0:T(8,128)(2,1)S(1)}, u32[]{:S(2)}) %copy-start.1) | copy-done | bytes 71704
  33.8 0.0 copy-start.2
  33.8 0.6 %copy-done.2 = bf16[2,35,512]{2,1,0:T(8,128)(2,1)} copy-done((bf16[2,35,512]{2,1,0:T(8,128)(2,1)}, bf16[2,35,512]{2,1,0:T(8,128)(2,1)S(1)}, u32[]{:S(2)}) %copy-start.2) | copy-done | bytes 71704
  34.4 13.5 %fine_step.1 = f32[35,2,8192]{2,1,0:T(2,128)} custom-call(f32[3]{0:T(128)} %velocity.3, f32[35,35]{1,0:T(8,128)} %stoich.3, f32[35]{0:T(128)} %diffusivity.3, bf16[256,2048]{1,0:T(8,128)(2,1)} %constant.8.clone.weights, bf16[2,35,512]{2,1,0:T(8,128)(2,1)} %copy-done.1, bf16[2,35,512]{2,1,0:T(8,128)(2,1)} %copy-done.2, ...), custom_call_target="tpu_custom_call" | custom-call | flops 4000000000 | bytes 8000000 | tf_op jit(solution)/shard_map/fine_step/pallas_call | solution.py:384
Async XLA Ops:
  0.6 6.6 %collective-permute-start = (bf16[1,35,1024]{2,1,0:T(8,128)(2,1)}, bf16[1,35,1024]{2,1,0:T(8,128)(2,1)S(1)}, u32[]{:S(2)}, u32[]{:S(2)}) collective-permute-start(bf16[1,35,1024]{2,1,0:T(8,128)(2,1)} %own.1), channel_id=1, source_target_pairs={{0,8},{4,12},{8,16},{12,20},{16,24},{20,28},{24,0},{28,4},{1,9},{5... | collective-permute-start | bytes 215048 | tf_op jit(solution)/shard_map/ppermute | solution.py:454
  2.8 8.7 %collective-permute-start.1 = (bf16[1,35,1024]{2,1,0:T(8,128)(2,1)}, bf16[1,35,1024]{2,1,0:T(8,128)(2,1)S(1)}, u32[]{:S(2)}, u32[]{:S(2)}) collective-permute-start(bf16[1,35,1024]{2,1,0:T(8,128)(2,1)} %own.1), channel_id=1, source_target_pairs={{0,16},{4,20},{8,24},{12,28},{16,0},{20,4},{24,8},{28,12},{1,17},{... | collective-permute-start | bytes 215048 | tf_op jit(solution)/shard_map/ppermute | solution.py:454
  5.1 6.3 %collective-permute-start.2 = (bf16[1,35,1024]{2,1,0:T(8,128)(2,1)}, bf16[1,35,1024]{2,1,0:T(8,128)(2,1)S(1)}, u32[]{:S(2)}, u32[]{:S(2)}) collective-permute-start(bf16[1,35,1024]{2,1,0:T(8,128)(2,1)} %own.1), channel_id=1, source_target_pairs={{0,24},{4,28},{8,0},{12,4},{16,8},{20,12},{24,16},{28,20},{1,25},{... | collective-permute-start | bytes 215048 | tf_op jit(solution)/shard_map/ppermute | solution.py:454
  7.2 4.3 %copy-start.3 = (bf16[1,35,1024]{2,1,0:T(8,128)(2,1)}, bf16[1,35,1024]{2,1,0:T(8,128)(2,1)S(1)}, u32[]{:S(2)}) copy-start(bf16[1,35,1024]{2,1,0:T(8,128)(2,1)S(1)} %collective-permute-done.refs_1_) | copy-start | bytes 215044
  11.5 0.6 %copy-start.4 = (bf16[1,35,1024]{2,1,0:T(8,128)(2,1)}, bf16[1,35,1024]{2,1,0:T(8,128)(2,1)S(1)}, u32[]{:S(2)}) copy-start(bf16[1,35,1024]{2,1,0:T(8,128)(2,1)S(1)} %collective-permute-done.1.refs_2_) | copy-start | bytes 215044
  12.1 0.6 %copy-start.5 = (bf16[1,35,1024]{2,1,0:T(8,128)(2,1)}, bf16[1,35,1024]{2,1,0:T(8,128)(2,1)S(1)}, u32[]{:S(2)}) copy-start(bf16[1,35,1024]{2,1,0:T(8,128)(2,1)S(1)} %collective-permute-done.2.refs_3_) | copy-start | bytes 215044
  14.6 7.9 %collective-permute-start.3 = (bf16[2,35,1024]{2,1,0:T(8,128)(2,1)}, bf16[2,35,1024]{2,1,0:T(8,128)(2,1)S(1)}, u32[]{:S(2)}, u32[]{:S(2)}) collective-permute-start(bf16[2,35,1024]{2,1,0:T(8,128)(2,1)} %get-tuple-element.5), channel_id=1, source_target_pairs={{0,4},{4,0},{8,12},{12,8},{16,20},{20,16},{24,28},{28,24},{1,5},{5... | collective-permute-start | bytes 430088 | tf_op jit(solution)/shard_map/ppermute | solution.py:468
  16.5 12.6 %collective-permute-start.6 = (bf16[1,35,512]{2,1,0:T(8,128)(2,1)S(1)}, bf16[1,35,512]{2,1,0:T(8,128)(2,1)S(1)}, u32[]{:S(2)}, u32[]{:S(2)}) collective-permute-start(bf16[1,35,512]{2,1,0:T(8,128)(2,1)S(1)} %get-tuple-element.9), channel_id=1, source_target_pairs={{0,1},{1,2},{2,3},{4,5},{5,6},{6,7},{8,9},{9,10},{10,11},{12,13},{... | collective-permute-start | bytes 107528 | tf_op jit(solution)/shard_map/ppermute | solution.py:443
  20.6 8.6 %collective-permute-start.7 = (bf16[1,35,512]{2,1,0:T(8,128)(2,1)S(1)}, bf16[1,35,512]{2,1,0:T(8,128)(2,1)S(1)}, u32[]{:S(2)}, u32[]{:S(2)}) collective-permute-start(bf16[1,35,512]{2,1,0:T(8,128)(2,1)S(1)} %get-tuple-element.8), channel_id=1, source_target_pairs={{1,0},{2,1},{3,2},{5,4},{6,5},{7,6},{9,8},{10,9},{11,10},{13,12},{... | collective-permute-start | bytes 107528 | tf_op jit(solution)/shard_map/ppermute | solution.py:443
  22.5 10.7 %copy-start = (bf16[2,35,1024]{2,1,0:T(8,128)(2,1)}, bf16[2,35,1024]{2,1,0:T(8,128)(2,1)S(1)}, u32[]{:S(2)}) copy-start(bf16[2,35,1024]{2,1,0:T(8,128)(2,1)S(1)} %collective-permute-done.3.refs_3_) | copy-start | bytes 430084
  23.5 9.6 %collective-permute-start.4 = (bf16[2,35,512]{2,1,0:T(8,128)(2,1)S(1)}, bf16[2,35,512]{2,1,0:T(8,128)(2,1)S(1)}, u32[]{:S(2)}, u32[]{:S(2)}) collective-permute-start(bf16[2,35,512]{2,1,0:T(8,128)(2,1)S(1)} %get-tuple-element.7), channel_id=1, source_target_pairs={{0,1},{1,2},{2,3},{4,5},{5,6},{6,7},{8,9},{9,10},{10,11},{12,13},{... | collective-permute-start | bytes 215048 | tf_op jit(solution)/shard_map/ppermute | solution.py:443
  27.2 6.0 %collective-permute-start.5 = (bf16[2,35,512]{2,1,0:T(8,128)(2,1)S(1)}, bf16[2,35,512]{2,1,0:T(8,128)(2,1)S(1)}, u32[]{:S(2)}, u32[]{:S(2)}) collective-permute-start(bf16[2,35,512]{2,1,0:T(8,128)(2,1)S(1)} %get-tuple-element.6), channel_id=1, source_target_pairs={{1,0},{2,1},{3,2},{5,4},{6,5},{7,6},{9,8},{10,9},{11,10},{13,12},{... | collective-permute-start | bytes 215048 | tf_op jit(solution)/shard_map/ppermute | solution.py:443
  29.1 0.6 %copy-start.6 = (bf16[1,35,512]{2,1,0:T(8,128)(2,1)}, bf16[1,35,512]{2,1,0:T(8,128)(2,1)S(1)}, u32[]{:S(2)}) copy-start(bf16[1,35,512]{2,1,0:T(8,128)(2,1)S(1)} %collective-permute-done.6.low) | copy-start | bytes 107524
  29.1 0.6 %copy-start.7 = (bf16[1,35,512]{2,1,0:T(8,128)(2,1)}, bf16[1,35,512]{2,1,0:T(8,128)(2,1)S(1)}, u32[]{:S(2)}) copy-start(bf16[1,35,512]{2,1,0:T(8,128)(2,1)S(1)} %collective-permute-done.7.high) | copy-start | bytes 107524
  33.2 0.6 %copy-start.1 = (bf16[2,35,512]{2,1,0:T(8,128)(2,1)}, bf16[2,35,512]{2,1,0:T(8,128)(2,1)S(1)}, u32[]{:S(2)}) copy-start(bf16[2,35,512]{2,1,0:T(8,128)(2,1)S(1)} %collective-permute-done.4.refs_0_) | copy-start | bytes 215044
  33.8 0.6 %copy-start.2 = (bf16[2,35,512]{2,1,0:T(8,128)(2,1)}, bf16[2,35,512]{2,1,0:T(8,128)(2,1)S(1)}, u32[]{:S(2)}) copy-start(bf16[2,35,512]{2,1,0:T(8,128)(2,1)S(1)} %collective-permute-done.5.refs_1_) | copy-start | bytes 215044
